TPU v7x, 512 devices: a whole 4x8x8 slice. The times are simulated.
512 devices in a mesh: seq: 64 (over y, z), head: 8 (over x, core).
Axes of the slice: x: 4, y: 8, z: 8, core: 2. Of those that a mesh axis runs over, the one named last changes fastest.
Arguments:
- queries: bfloat16 [16384, 1024], P('seq', 'head'), may hold values from -5 to 5
- key_rows: bfloat16 [16384, 1024], P('seq', 'head'), may hold values from -5 to 5
- value_rows: bfloat16 [16384, 1024], P('seq', 'head'), may hold values from -6 to 6
- key_blocks: int32 [256, 9], P('seq'), may hold values from -1 to 254, as said below
- out_weight: bfloat16 [1024, 1024], P('head'), may hold values from -0.1875 to 0.1875
- grad_out: bfloat16 [16384, 1024], P('seq', 'head'), may hold values from -6 to 6
Outputs:
- mixed: bfloat16 [16384, 1024], P('seq', 'head')
- grad_queries: bfloat16 [16384, 1024], P('seq', 'head')
- grad_keys: bfloat16 [16384, 1024], P('seq', 'head')
- grad_values: bfloat16 [16384, 1024], P('seq', 'head')
Inputs may be any that keep to these rules, and one draw needn't show every extreme that they name: key_blocks[q, j] is either q - 2**j or -1; it is -1 wherever q < 2**j, and never -1 for j = 0 and q >= 1.
All inputs are finite; a program needn't handle non-finite values.
Results may differ from a plain program's by a relative error of at most 0.03.
Values may be sent and summed in bfloat16 or wider, within the bound.
A program may use at most 64 MiB of HBM per device.

v0:
```python
import jax
import jax.numpy as jnp
from jax import lax
from jax.sharding import PartitionSpec as P

HD = 128
BLOCK = 64
LEVELS = 9


def shifted(value, axis, steps):
    count = lax.axis_size(axis)
    initial, last = (max(0, -steps), min(count, count - steps))
    return lax.ppermute(value, axis, [(source, source + steps) for source in range(initial, last)])


def per_device(queries, key_rows, value_rows, key_blocks, out_weight, grad_out):
    tok_rows, local_width = queries.shape
    head_count = local_width // HD
    block_count = tok_rows // BLOCK
    seq_count = lax.axis_size("seq")
    total_blocks = block_count * seq_count
    offsets = [2**power for power in range(LEVELS) if 2**power < total_blocks]
    nearby = [stride for stride in offsets if stride < block_count]
    distant = [stride // block_count for stride in offsets if stride >= block_count]
    farthest = max(nearby)
    tail_rows = farthest * BLOCK
    packed = jnp.stack([key_rows, value_rows])
    fetched = [packed]
    tail = shifted(packed[:, tok_rows - tail_rows :], "seq", 1)
    for stride in nearby:
        fetched.append(
            jnp.concatenate(
                [tail[:, (farthest - stride) * BLOCK :], packed[:, : tok_rows - stride * BLOCK]],
                axis=1,
            )
        )
    for distance in distant:
        fetched.append(shifted(packed, "seq", distance))
    grad_attn = lax.dot_general(
        lax.all_gather(grad_out, "head", axis=1, tiled=True),
        out_weight,
        (((1,), (1,)), ((), ())),
        preferred_element_type=jnp.float32,
    ).astype(jnp.bfloat16)
    scaling = HD ** (-0.5)

    def to_blocks(array):
        return array.reshape(block_count, BLOCK, head_count, HD)

    def column_band(array, ordinal):
        return array[..., ordinal * BLOCK : (ordinal + 1) * BLOCK]

    query_blocks = to_blocks(queries)
    grad_blocks = to_blocks(grad_attn)
    causal = jnp.arange(BLOCK)[:, None] >= jnp.arange(BLOCK)[None, :]
    pieces = []
    for ordinal, source in enumerate(fetched):
        partial_scores = (
            jnp.einsum(
                "jqhd,jkhd->jhqk",
                query_blocks,
                to_blocks(source[0]),
                preferred_element_type=jnp.float32,
            )
            * scaling
        )
        if ordinal == 0:
            allowed = causal[None, None]
        else:
            allowed = (key_blocks[:, ordinal - 1] >= 0)[:, None, None, None]
        pieces.append(jnp.where(allowed, partial_scores, -1e30))
    scores = jnp.concatenate(pieces, axis=-1)
    highest = jnp.max(scores, axis=-1, keepdims=True)
    log_total = highest + jnp.log(jnp.sum(jnp.exp(scores - highest), axis=-1, keepdims=True))
    probs = jnp.exp(scores - log_total)
    probs_b = probs.astype(jnp.bfloat16)
    attn = jnp.zeros((block_count, BLOCK, head_count, HD), jnp.float32)
    for ordinal, source in enumerate(fetched):
        attn = attn + jnp.einsum(
            "jhqk,jkhd->jqhd",
            column_band(probs_b, ordinal),
            to_blocks(source[1]),
            preferred_element_type=jnp.float32,
        )
    attn = attn.reshape(tok_rows, local_width).astype(jnp.bfloat16)
    products = jnp.dot(attn, out_weight, preferred_element_type=jnp.float32)
    mixed = lax.psum_scatter(products.astype(jnp.bfloat16), "head", scatter_dimension=1, tiled=True)
    row_inner = jnp.einsum(
        "jqhd,jqhd->jhq", grad_blocks, to_blocks(attn), preferred_element_type=jnp.float32
    )
    grad_probs = jnp.concatenate(
        [
            jnp.einsum(
                "jqhd,jkhd->jhqk",
                grad_blocks,
                to_blocks(source[1]),
                preferred_element_type=jnp.float32,
            )
            for source in fetched
        ],
        axis=-1,
    )
    grad_scores = (probs * (grad_probs - row_inner[..., None]) * scaling).astype(jnp.bfloat16)
    grad_queries = jnp.zeros((block_count, BLOCK, head_count, HD), jnp.float32)
    contribs = []
    for ordinal, source in enumerate(fetched):
        band_scores = column_band(grad_scores, ordinal)
        grad_queries = grad_queries + jnp.einsum(
            "jhqk,jkhd->jqhd", band_scores, to_blocks(source[0]), preferred_element_type=jnp.float32
        )
        key_part = jnp.einsum(
            "jhqk,jqhd->jkhd", band_scores, query_blocks, preferred_element_type=jnp.float32
        )
        value_part = jnp.einsum(
            "jhqk,jqhd->jkhd",
            column_band(probs_b, ordinal),
            grad_blocks,
            preferred_element_type=jnp.float32,
        )
        contribs.append(jnp.stack([key_part, value_part]).reshape(2, tok_rows, local_width))
    grad_queries = grad_queries.reshape(tok_rows, local_width).astype(jnp.bfloat16)
    gathered = contribs[0]
    tail_sum = jnp.zeros((2, tail_rows, local_width), jnp.float32)
    for ordinal, stride in enumerate(nearby):
        contrib = contribs[1 + ordinal]
        cut = stride * BLOCK
        gathered = gathered + jnp.pad(contrib[:, cut:], ((0, 0), (0, cut), (0, 0)))
        tail_sum = tail_sum + jnp.pad(contrib[:, :cut], ((0, 0), (tail_rows - cut, 0), (0, 0)))
    far_terms = contribs[1 + len(nearby) :]
    for distance, contrib in zip(distant, far_terms):
        gathered = gathered + shifted(contrib.astype(jnp.bfloat16), "seq", -distance).astype(
            contrib.dtype
        )
    returned = shifted(tail_sum.astype(jnp.bfloat16), "seq", -1).astype(tail_sum.dtype)
    gathered = gathered + jnp.pad(returned, ((0, 0), (tok_rows - tail_rows, 0), (0, 0)))
    return (mixed, grad_queries, gathered[0].astype(jnp.bfloat16), gathered[1].astype(jnp.bfloat16))


def solution(mesh):
    in_specs = (
        P("seq", "head"),
        P("seq", "head"),
        P("seq", "head"),
        P("seq", None),
        P("head", None),
        P("seq", "head"),
    )
    out_specs = (P("seq", "head"), P("seq", "head"), P("seq", "head"), P("seq", "head"))
    return jax.shard_map(
        per_device, mesh=mesh, in_specs=in_specs, out_specs=out_specs, check_vma=False
    )
```

profile of v0, /device:TPU:32, one launch (start us, length us, event | category | flops | bytes accessed | tf_op | source)
XLA Modules:
  0.0 134.0 jit_solution(10727877855267440195)
XLA Ops:
  7.2 0.9 pad_maximum_fusion
  8.2 1.3 collective-permute-start.6
  9.5 4.3 %collective-permute-start.1 = (bf16[2,256,128]{2,1,0:T(8,128)(2,1)S(1)}, bf16[2,256,128]{2,1,0:T(8,128)(2,1)S(1)}, u32[]{:S(2)}, u32[]{:S(2)}) collective-permute-start(bf16[2,256,128]{2,1,0:T(8,128)(2,1)S(1)} %pad_maximum_fusion), channel_id=1, source_target_pairs={{0,8},{8,16},{16,24},{24,32},{32,40},{40,48},{48,56},{56,64},{64,7... | collective-permute-start | bytes 393224 | tf_op jit(solution)/shard_map/ppermute | solution.py:14
  13.8 6.1 %collective-permute-start.2 = (bf16[2,256,128]{2,1,0:T(8,128)(2,1)S(1)}, bf16[2,256,128]{2,1,0:T(8,128)(2,1)S(1)}, u32[]{:S(2)}, u32[]{:S(2)}) collective-permute-start(bf16[2,256,128]{2,1,0:T(8,128)(2,1)S(1)} %pad_maximum_fusion), channel_id=1, source_target_pairs={{0,16},{8,24},{16,32},{24,40},{32,48},{40,56},{48,64},{56,72},{64,... | collective-permute-start | bytes 393224 | tf_op jit(solution)/shard_map/ppermute | solution.py:14
  19.9 8.2 %collective-permute-start.3 = (bf16[2,256,128]{2,1,0:T(8,128)(2,1)S(1)}, bf16[2,256,128]{2,1,0:T(8,128)(2,1)S(1)}, u32[]{:S(2)}, u32[]{:S(2)}) collective-permute-start(bf16[2,256,128]{2,1,0:T(8,128)(2,1)S(1)} %pad_maximum_fusion), channel_id=1, source_target_pairs={{0,32},{8,40},{16,48},{24,56},{32,64},{40,72},{48,80},{56,88},{64,... | collective-permute-start | bytes 393224 | tf_op jit(solution)/shard_map/ppermute | solution.py:14
  28.2 1.9 %collective-permute-start = (bf16[2,128,128]{2,1,0:T(8,128)(2,1)S(1)}, bf16[2,128,128]{2,1,0:T(8,128)(2,1)S(1)}, u32[]{:S(2)}, u32[]{:S(2)}) collective-permute-start(bf16[2,128,128]{2,1,0:T(8,128)(2,1)S(1)} %get-tuple-element.33), channel_id=1, source_target_pairs={{0,8},{8,16},{16,24},{24,32},{32,40},{40,48},{48,56},{56,64},{64,7... | collective-permute-start | bytes 196616 | tf_op jit(solution)/shard_map/ppermute | solution.py:14
  30.1 0.8 copy-done.14
  30.9 13.0 %all_gather.3 = bf16[256,1024]{1,0:T(8,128)(2,1)S(1)} all-gather(bf16[256,128]{1,0:T(8,128)(2,1)S(1)} %copy-done.14), channel_id=1, replica_groups=mesh['seq'=64,'head'=8] {'head'}, dimensions={1}, use_global_device_ids=true | all-gather | bytes 589824 | tf_op jit(solution)/shard_map/all_gather | solution.py:41
  43.9 0.3 convolution_convert_fusion.1
  44.4 0.7 copy-done.1
  45.3 0.4 copy-done.13
  46.1 2.6 %collective-permute-start.4 = (bf16[2,256,128]{2,1,0:T(8,128)(2,1)S(1)}, bf16[2,256,128]{2,1,0:T(8,128)(2,1)S(1)}, u32[]{:S(2)}, u32[]{:S(2)}) collective-permute-start(bf16[2,256,128]{2,1,0:T(8,128)(2,1)S(1)} %pad_maximum_fusion), channel_id=1, source_target_pairs={{0,64},{8,72},{16,80},{24,88},{32,96},{40,104},{48,112},{56,120},{... | collective-permute-start | bytes 393224 | tf_op jit(solution)/shard_map/ppermute | solution.py:14
  49.5 2.7 %collective-permute-start.5 = (bf16[2,256,128]{2,1,0:T(8,128)(2,1)S(1)}, bf16[2,256,128]{2,1,0:T(8,128)(2,1)S(1)}, u32[]{:S(2)}, u32[]{:S(2)}) collective-permute-start(bf16[2,256,128]{2,1,0:T(8,128)(2,1)S(1)} %pad_maximum_fusion), channel_id=1, source_target_pairs={{0,128},{8,136},{16,144},{24,152},{32,160},{40,168},{48,176},{56,1... | collective-permute-start | bytes 393224 | tf_op jit(solution)/shard_map/ppermute | solution.py:14
  53.1 3.2 %collective-permute-done.4 = bf16[2,256,128]{2,1,0:T(8,128)(2,1)S(1)} collective-permute-done((bf16[2,256,128]{2,1,0:T(8,128)(2,1)S(1)}, bf16[2,256,128]{2,1,0:T(8,128)(2,1)S(1)}, u32[]{:S(2)}, u32[]{:S(2)}) %collective-permute-start.4) | collective-permute-done | bytes 131104 | tf_op jit(solution)/shard_map/ppermute | solution.py:14
  56.3 0.8 bitcast_reduce_fusion.2
  57.2 4.5 %collective-permute-done.5 = bf16[2,256,128]{2,1,0:T(8,128)(2,1)S(1)} collective-permute-done((bf16[2,256,128]{2,1,0:T(8,128)(2,1)S(1)}, bf16[2,256,128]{2,1,0:T(8,128)(2,1)S(1)}, u32[]{:S(2)}, u32[]{:S(2)}) %collective-permute-start.5) | collective-permute-done | bytes 131104 | tf_op jit(solution)/shard_map/ppermute | solution.py:14
  61.7 0.8 bitcast_reduce_fusion.1
  62.5 0.8 bitcast_reduce_fusion
  63.3 1.3 concatenate.102
  65.8 0.8 convolution_bitcast_fusion.5
  66.8 0.8 convolution_bitcast_fusion.4
  67.8 0.8 convolution_bitcast_fusion.3
  68.8 0.8 convolution_bitcast_fusion.2
  69.8 0.8 convolution_bitcast_fusion.1
  70.8 0.8 fusion.36
  71.7 1.4 %concatenate.112 = f32[4,1,64,576]{3,2,0,1:T(8,128)S(1)} concatenate(f32[4,1,64,64]{3,2,0,1:T(8,128)S(1)} %convolution_bitcast_fusion.9, f32[4,1,64,64]{3,2,0,1:T(8,128)S(1)} %convolution_bitcast_fusion.8, f32[4,1,64,64]{3,2,0,1:T(8,128)S(1)} %convolution_bitcast_fusion.7, f32[4,1,64,64]{3,2,0,1:T(8,128)S(1)} %convolution_bitcast_fusion.6, f32[4,1,64,64]{3,2,0,1:T(8,128)S(1)} %copy-done.4, ...), dimensions={3} | concatenate | bytes 1179648 | tf_op jit(solution)/shard_map/concatenate | solution.py:92
  74.6 0.9 convolution_convert_fusion.2
  75.4 0.8 convolution_convert_fusion.3
  76.3 0.9 convolution_convert_fusion.4
  77.2 0.9 convolution_convert_fusion.5
  78.1 0.8 convolution_convert_fusion.6
  78.9 0.8 convolution_convert_fusion.7
  80.0 0.9 convolution_convert_fusion.9
  82.9 0.6 copy-done.12
  83.8 1.0 copy.73
  85.2 0.7 copy-done.10
  85.9 2.4 %collective-permute-start.12 = (bf16[2,256,128]{2,1,0:T(8,128)(2,1)S(1)}, bf16[2,256,128]{2,1,0:T(8,128)(2,1)S(1)}, u32[]{:S(2)}, u32[]{:S(2)}) collective-permute-start(bf16[2,256,128]{2,1,0:T(8,128)(2,1)S(1)} %pad_maximum_fusion.7), channel_id=1, source_target_pairs={{256,0},{264,8},{272,16},{280,24},{288,32},{296,40},{304,48},{312,... | collective-permute-start | bytes 393224 | tf_op jit(solution)/shard_map/ppermute | solution.py:14
  88.4 2.5 %collective-permute-start.11 = (bf16[2,256,128]{2,1,0:T(8,128)(2,1)S(1)}, bf16[2,256,128]{2,1,0:T(8,128)(2,1)S(1)}, u32[]{:S(2)}, u32[]{:S(2)}) collective-permute-start(bf16[2,256,128]{2,1,0:T(8,128)(2,1)S(1)} %pad_maximum_fusion.6), channel_id=1, source_target_pairs={{128,0},{136,8},{144,16},{152,24},{160,32},{168,40},{176,48},{184,... | collective-permute-start | bytes 393224 | tf_op jit(solution)/shard_map/ppermute | solution.py:14
  90.9 3.5 %collective-permute-start.10 = (bf16[2,256,128]{2,1,0:T(8,128)(2,1)S(1)}, bf16[2,256,128]{2,1,0:T(8,128)(2,1)S(1)}, u32[]{:S(2)}, u32[]{:S(2)}) collective-permute-start(bf16[2,256,128]{2,1,0:T(8,128)(2,1)S(1)} %pad_maximum_fusion.5), channel_id=1, source_target_pairs={{64,0},{72,8},{80,16},{88,24},{96,32},{104,40},{112,48},{120,56},{... | collective-permute-start | bytes 393224 | tf_op jit(solution)/shard_map/ppermute | solution.py:14
  94.5 4.5 %collective-permute-start.9 = (bf16[2,256,128]{2,1,0:T(8,128)(2,1)S(1)}, bf16[2,256,128]{2,1,0:T(8,128)(2,1)S(1)}, u32[]{:S(2)}, u32[]{:S(2)}) collective-permute-start(bf16[2,256,128]{2,1,0:T(8,128)(2,1)S(1)} %pad_maximum_fusion.4), channel_id=1, source_target_pairs={{32,0},{40,8},{48,16},{56,24},{64,32},{72,40},{80,48},{88,56},{96,... | collective-permute-start | bytes 393224 | tf_op jit(solution)/shard_map/ppermute | solution.py:14
  99.0 2.0 %collective-permute-start.13 = (bf16[2,128,128]{2,1,0:T(8,128)(2,1)S(1)}, bf16[2,128,128]{2,1,0:T(8,128)(2,1)S(1)}, u32[]{:S(2)}, u32[]{:S(2)}) collective-permute-start(bf16[2,128,128]{2,1,0:T(8,128)(2,1)S(1)} %get-tuple-element.12), channel_id=1, source_target_pairs={{8,0},{16,8},{24,16},{32,24},{40,32},{48,40},{56,48},{64,56},{72,6... | collective-permute-start | bytes 196616 | tf_op jit(solution)/shard_map/ppermute | solution.py:14
  101.0 0.9 fusion.20
  101.9 8.2 %collective-permute-done.13 = bf16[2,128,128]{2,1,0:T(8,128)(2,1)S(1)} collective-permute-done((bf16[2,128,128]{2,1,0:T(8,128)(2,1)S(1)}, bf16[2,128,128]{2,1,0:T(8,128)(2,1)S(1)}, u32[]{:S(2)}, u32[]{:S(2)}) %collective-permute-start.13) | collective-permute-done | bytes 65568 | tf_op jit(solution)/shard_map/ppermute | solution.py:14
  110.1 1.9 %collective-permute-start.8 = (bf16[2,256,128]{2,1,0:T(8,128)(2,1)S(1)}, bf16[2,256,128]{2,1,0:T(8,128)(2,1)S(1)}, u32[]{:S(2)}, u32[]{:S(2)}) collective-permute-start(bf16[2,256,128]{2,1,0:T(8,128)(2,1)S(1)} %pad_maximum_fusion.3), channel_id=1, source_target_pairs={{16,0},{24,8},{32,16},{40,24},{48,32},{56,40},{64,48},{72,56},{80,... | collective-permute-start | bytes 393224 | tf_op jit(solution)/shard_map/ppermute | solution.py:14
  112.0 8.3 %collective-permute-start.7 = (bf16[2,256,128]{2,1,0:T(8,128)(2,1)S(1)}, bf16[2,256,128]{2,1,0:T(8,128)(2,1)S(1)}, u32[]{:S(2)}, u32[]{:S(2)}) collective-permute-start(bf16[2,256,128]{2,1,0:T(8,128)(2,1)S(1)} %pad_maximum_fusion.2), channel_id=1, source_target_pairs={{8,0},{16,8},{24,16},{32,24},{40,32},{48,40},{56,48},{64,56},{72,6... | collective-permute-start | bytes 393224 | tf_op jit(solution)/shard_map/ppermute | solution.py:14
  120.6 4.1 %collective-permute-done.7 = bf16[2,256,128]{2,1,0:T(8,128)(2,1)S(1)} collective-permute-done((bf16[2,256,128]{2,1,0:T(8,128)(2,1)S(1)}, bf16[2,256,128]{2,1,0:T(8,128)(2,1)S(1)}, u32[]{:S(2)}, u32[]{:S(2)}) %collective-permute-start.7) | collective-permute-done | bytes 131104 | tf_op jit(solution)/shard_map/ppermute | solution.py:14
  124.9 0.7 slice_bitcast_fusion
  125.5 1.6 %copy.74 = bf16[256,128]{1,0:T(8,128)(2,1)} copy(bf16[256,128]{0,1:T(8,128)(2,1)} %bitcast.464) | data formatting | bytes 131072
  (103 shorter events, 9.4 us)
Async XLA Ops:
  7.2 36.7 %copy-start = (bf16[128,1024]{1,0:T(8,128)(2,1)S(1)}, bf16[128,1024]{1,0:T(8,128)(2,1)}, u32[]{:S(2)}) copy-start(bf16[128,1024]{1,0:T(8,128)(2,1)} %param.10) | copy-start | bytes 786436
  7.2 118.4 %reduce-scatter.4.cloned.1.call-start = ((), (), s32[]{:S(2)}) async-start(), calls=%async_computation.1 | async-start | bytes 589824
  7.2 20.9 %copy-start.2 = (bf16[256,128]{1,0:T(8,128)(2,1)S(1)}, bf16[256,128]{1,0:T(8,128)(2,1)}, u32[]{:S(2)}) copy-start(bf16[256,128]{1,0:T(8,128)(2,1)} %param.8) | copy-start | bytes 196612
  7.2 20.9 %copy-start.3 = (bf16[256,128]{1,0:T(8,128)(2,1)S(1)}, bf16[256,128]{1,0:T(8,128)(2,1)}, u32[]{:S(2)}) copy-start(bf16[256,128]{1,0:T(8,128)(2,1)} %param.7) | copy-start | bytes 196612
  8.2 54.3 %collective-permute-start.6 = (bf16[2,256,128]{2,1,0:T(8,128)(2,1)S(1)}, bf16[2,256,128]{2,1,0:T(8,128)(2,1)S(1)}, u32[]{:S(2)}, u32[]{:S(2)}) collective-permute-start(bf16[2,256,128]{2,1,0:T(8,128)(2,1)S(1)} %pad_maximum_fusion), channel_id=1, source_target_pairs={{0,256},{8,264},{16,272},{24,280},{32,288},{40,296},{48,304},{56,3... | collective-permute-start | bytes 393224 | tf_op jit(solution)/shard_map/ppermute | solution.py:14
  9.5 40.0 %collective-permute-start.1 = (bf16[2,256,128]{2,1,0:T(8,128)(2,1)S(1)}, bf16[2,256,128]{2,1,0:T(8,128)(2,1)S(1)}, u32[]{:S(2)}, u32[]{:S(2)}) collective-permute-start(bf16[2,256,128]{2,1,0:T(8,128)(2,1)S(1)} %pad_maximum_fusion), channel_id=1, source_target_pairs={{0,8},{8,16},{16,24},{24,32},{32,40},{40,48},{48,56},{56,64},{64,7... | collective-permute-start | bytes 393224 | tf_op jit(solution)/shard_map/ppermute | solution.py:14
  13.8 38.7 %collective-permute-start.2 = (bf16[2,256,128]{2,1,0:T(8,128)(2,1)S(1)}, bf16[2,256,128]{2,1,0:T(8,128)(2,1)S(1)}, u32[]{:S(2)}, u32[]{:S(2)}) collective-permute-start(bf16[2,256,128]{2,1,0:T(8,128)(2,1)S(1)} %pad_maximum_fusion), channel_id=1, source_target_pairs={{0,16},{8,24},{16,32},{24,40},{32,48},{40,56},{48,64},{56,72},{64,... | collective-permute-start | bytes 393224 | tf_op jit(solution)/shard_map/ppermute | solution.py:14
  19.9 32.9 %collective-permute-start.3 = (bf16[2,256,128]{2,1,0:T(8,128)(2,1)S(1)}, bf16[2,256,128]{2,1,0:T(8,128)(2,1)S(1)}, u32[]{:S(2)}, u32[]{:S(2)}) collective-permute-start(bf16[2,256,128]{2,1,0:T(8,128)(2,1)S(1)} %pad_maximum_fusion), channel_id=1, source_target_pairs={{0,32},{8,40},{16,48},{24,56},{32,64},{40,72},{48,80},{56,88},{64,... | collective-permute-start | bytes 393224 | tf_op jit(solution)/shard_map/ppermute | solution.py:14
  28.2 17.9 %collective-permute-start = (bf16[2,128,128]{2,1,0:T(8,128)(2,1)S(1)}, bf16[2,128,128]{2,1,0:T(8,128)(2,1)S(1)}, u32[]{:S(2)}, u32[]{:S(2)}) collective-permute-start(bf16[2,128,128]{2,1,0:T(8,128)(2,1)S(1)} %get-tuple-element.33), channel_id=1, source_target_pairs={{0,8},{8,16},{16,24},{24,32},{32,40},{40,48},{48,56},{56,64},{64,7... | collective-permute-start | bytes 196616 | tf_op jit(solution)/shard_map/ppermute | solution.py:14
  30.1 0.8 copy-start.14
  44.2 0.8 copy-start.1
  45.1 0.7 copy-start.13
  46.1 10.3 %collective-permute-start.4 = (bf16[2,256,128]{2,1,0:T(8,128)(2,1)S(1)}, bf16[2,256,128]{2,1,0:T(8,128)(2,1)S(1)}, u32[]{:S(2)}, u32[]{:S(2)}) collective-permute-start(bf16[2,256,128]{2,1,0:T(8,128)(2,1)S(1)} %pad_maximum_fusion), channel_id=1, source_target_pairs={{0,64},{8,72},{16,80},{24,88},{32,96},{40,104},{48,112},{56,120},{... | collective-permute-start | bytes 393224 | tf_op jit(solution)/shard_map/ppermute | solution.py:14
  49.5 12.1 %collective-permute-start.5 = (bf16[2,256,128]{2,1,0:T(8,128)(2,1)S(1)}, bf16[2,256,128]{2,1,0:T(8,128)(2,1)S(1)}, u32[]{:S(2)}, u32[]{:S(2)}) collective-permute-start(bf16[2,256,128]{2,1,0:T(8,128)(2,1)S(1)} %pad_maximum_fusion), channel_id=1, source_target_pairs={{0,128},{8,136},{16,144},{24,152},{32,160},{40,168},{48,176},{56,1... | collective-permute-start | bytes 393224 | tf_op jit(solution)/shard_map/ppermute | solution.py:14
  70.8 0.9 copy-start.4
  82.6 0.9 copy-start.12
  85.0 0.8 copy-start.10
  85.0 0.9 copy-start.11
  85.9 2.4 %copy-start.8 = (bf16[4,128,64]{1,2,0:T(8,128)(2,1)S(1)}, bf16[4,128,64]{1,2,0:T(8,128)(2,1)}, u32[]{:S(2)}) copy-start(bf16[4,128,64]{1,2,0:T(8,128)(2,1)} %convolution_convert_fusion.4) | copy-start | bytes 196612
  85.9 2.4 %copy-start.9 = (bf16[4,64,128]{2,1,0:T(8,128)(2,1)S(1)}, bf16[4,64,128]{2,1,0:T(8,128)(2,1)}, u32[]{:S(2)}) copy-start(bf16[4,64,128]{2,1,0:T(8,128)(2,1)} %convolution_convert_fusion.5) | copy-start | bytes 196612
  85.9 26.1 %collective-permute-start.12 = (bf16[2,256,128]{2,1,0:T(8,128)(2,1)S(1)}, bf16[2,256,128]{2,1,0:T(8,128)(2,1)S(1)}, u32[]{:S(2)}, u32[]{:S(2)}) collective-permute-start(bf16[2,256,128]{2,1,0:T(8,128)(2,1)S(1)} %pad_maximum_fusion.7), channel_id=1, source_target_pairs={{256,0},{264,8},{272,16},{280,24},{288,32},{296,40},{304,48},{312,... | collective-permute-start | bytes 393224 | tf_op jit(solution)/shard_map/ppermute | solution.py:14
  88.3 2.6 %copy-start.6 = (bf16[4,128,64]{1,2,0:T(8,128)(2,1)S(1)}, bf16[4,128,64]{1,2,0:T(8,128)(2,1)}, u32[]{:S(2)}) copy-start(bf16[4,128,64]{1,2,0:T(8,128)(2,1)} %convolution_convert_fusion.6) | copy-start | bytes 196612
  88.3 2.6 %copy-start.7 = (bf16[4,64,128]{2,1,0:T(8,128)(2,1)S(1)}, bf16[4,64,128]{2,1,0:T(8,128)(2,1)}, u32[]{:S(2)}) copy-start(bf16[4,64,128]{2,1,0:T(8,128)(2,1)} %convolution_convert_fusion.7) | copy-start | bytes 196612
  88.4 32.2 %collective-permute-start.11 = (bf16[2,256,128]{2,1,0:T(8,128)(2,1)S(1)}, bf16[2,256,128]{2,1,0:T(8,128)(2,1)S(1)}, u32[]{:S(2)}, u32[]{:S(2)}) collective-permute-start(bf16[2,256,128]{2,1,0:T(8,128)(2,1)S(1)} %pad_maximum_fusion.6), channel_id=1, source_target_pairs={{128,0},{136,8},{144,16},{152,24},{160,32},{168,40},{176,48},{184,... | collective-permute-start | bytes 393224 | tf_op jit(solution)/shard_map/ppermute | solution.py:14
  90.9 3.5 %copy-start.5 = (bf16[4,64,128]{2,1,0:T(8,128)(2,1)S(1)}, bf16[4,64,128]{2,1,0:T(8,128)(2,1)}, u32[]{:S(2)}) copy-start(bf16[4,64,128]{2,1,0:T(8,128)(2,1)} %convolution_convert_fusion.9) | copy-start | bytes 196612
  90.9 29.7 %collective-permute-start.10 = (bf16[2,256,128]{2,1,0:T(8,128)(2,1)S(1)}, bf16[2,256,128]{2,1,0:T(8,128)(2,1)S(1)}, u32[]{:S(2)}, u32[]{:S(2)}) collective-permute-start(bf16[2,256,128]{2,1,0:T(8,128)(2,1)S(1)} %pad_maximum_fusion.5), channel_id=1, source_target_pairs={{64,0},{72,8},{80,16},{88,24},{96,32},{104,40},{112,48},{120,56},{... | collective-permute-start | bytes 393224 | tf_op jit(solution)/shard_map/ppermute | solution.py:14
  94.5 26.1 %collective-permute-start.9 = (bf16[2,256,128]{2,1,0:T(8,128)(2,1)S(1)}, bf16[2,256,128]{2,1,0:T(8,128)(2,1)S(1)}, u32[]{:S(2)}, u32[]{:S(2)}) collective-permute-start(bf16[2,256,128]{2,1,0:T(8,128)(2,1)S(1)} %pad_maximum_fusion.4), channel_id=1, source_target_pairs={{32,0},{40,8},{48,16},{56,24},{64,32},{72,40},{80,48},{88,56},{96,... | collective-permute-start | bytes 393224 | tf_op jit(solution)/shard_map/ppermute | solution.py:14
  99.0 11.1 %collective-permute-start.13 = (bf16[2,128,128]{2,1,0:T(8,128)(2,1)S(1)}, bf16[2,128,128]{2,1,0:T(8,128)(2,1)S(1)}, u32[]{:S(2)}, u32[]{:S(2)}) collective-permute-start(bf16[2,128,128]{2,1,0:T(8,128)(2,1)S(1)} %get-tuple-element.12), channel_id=1, source_target_pairs={{8,0},{16,8},{24,16},{32,24},{40,32},{48,40},{56,48},{64,56},{72,6... | collective-permute-start | bytes 196616 | tf_op jit(solution)/shard_map/ppermute | solution.py:14
  110.1 10.5 %collective-permute-start.8 = (bf16[2,256,128]{2,1,0:T(8,128)(2,1)S(1)}, bf16[2,256,128]{2,1,0:T(8,128)(2,1)S(1)}, u32[]{:S(2)}, u32[]{:S(2)}) collective-permute-start(bf16[2,256,128]{2,1,0:T(8,128)(2,1)S(1)} %pad_maximum_fusion.3), channel_id=1, source_target_pairs={{16,0},{24,8},{32,16},{40,24},{48,32},{56,40},{64,48},{72,56},{80,... | collective-permute-start | bytes 393224 | tf_op jit(solution)/shard_map/ppermute | solution.py:14
  112.0 12.7 %collective-permute-start.7 = (bf16[2,256,128]{2,1,0:T(8,128)(2,1)S(1)}, bf16[2,256,128]{2,1,0:T(8,128)(2,1)S(1)}, u32[]{:S(2)}, u32[]{:S(2)}) collective-permute-start(bf16[2,256,128]{2,1,0:T(8,128)(2,1)S(1)} %pad_maximum_fusion.2), channel_id=1, source_target_pairs={{8,0},{16,8},{24,16},{32,24},{40,32},{48,40},{56,48},{64,56},{72,6... | collective-permute-start | bytes 393224 | tf_op jit(solution)/shard_map/ppermute | solution.py:14
Sparse Core Ops, SparseCore 0:
  84.9 34.3 reduce-scatter.3
where the time goes:
time: 135 us; the launch traced here: 134 us
  starting transfers between devices  52.2 us (39%)
  matrix products  22.5 us (17%)
  waiting for transfers between devices  20.1 us (15%)
  between operations  14.7 us (11%)
  blocking collectives  13 us (10%)
  local copies, waits for them, and re-layouts  9.33 us (7%)
  other arithmetic  2.22 us (2%)
    ppermute x14, starting transfers between devices, shifted(): lax.ppermute(value, axis, [(source, source + steps) for source in range(i...  52.2 us
    ppermute x14, waiting for transfers between devices, shifted(): lax.ppermute(value, axis, [(source, source + steps) for source in range(i...  20 us
    all_gather x1, blocking collectives, per_device(): lax.all_gather(grad_out, 'head', axis=1, tiled=True)  13 us
    unnamed x32, local copies, waits for them, and re-layouts  5.9 us
    dot_general x9, matrix products, per_device(): jnp.einsum('jqhd,jkhd->jhqk', grad_blocks, to_blocks(source[1]), preferre...  4.7 us
    dot_general x9, matrix products, per_device(): jnp.einsum('jhqk,jqhd->jkhd', band_scores, query_blocks, preferred_elemen...  4.67 us
    dot_general x9, matrix products, per_device(): jnp.einsum('jhqk,jqhd->jkhd', column_band(probs_b, ordinal), grad_blocks,...  4.07 us
    dot_general x9, matrix products, per_device(): jnp.einsum('jqhd,jkhd->jhqk', query_blocks, to_blocks(source[0]), preferr...  3.98 us
  transfers between devices with their start and end apart: 15, of which 4 were waited for; matrix products, arithmetic and copies ran while one was open for 5% of the time, Pallas kernels for 0%

commit v1 on v0

v1 whole, which is shorter than its diff:
```python
import functools

import jax
import jax.numpy as jnp
from jax import lax
from jax.experimental import pallas as pl
from jax.experimental.pallas import tpu as pltpu
from jax.sharding import PartitionSpec as P

HD = 128
BLOCK = 64
LEVELS = 9
ROW_CHIPS = 8
MESH = pl.DeviceIdType.MESH
BIG = 1e30


def dot_nt(a, b):
    return lax.dot_general(a, b, (((1,), (1,)), ((), ())), preferred_element_type=jnp.float32)


def dot_nn(a, b):
    return lax.dot_general(a, b, (((1,), (0,)), ((), ())), preferred_element_type=jnp.float32)


def kernel(
    n_seq, n_head, dists,
    q_hbm, k_hbm, v_hbm, kb_ref, w_hbm, g_hbm,
    mixed_ref, dq_ref, dk_ref, dv_ref,
    k_all, v_all, q_all, g_all, g_full, w_own, w_col, a_full, stat_mine, stat_got,
    seq_send, seq_recv, head_send, head_recv, stat_send, stat_recv, load_sem,
):
    seq = lax.axis_index("seq")
    head = lax.axis_index("head")
    nb = q_hbm.shape[0]
    slot_of = {dist: 1 + number for number, dist in enumerate(dists)}
    n_dist = len(dists)
    starts = [dist for dist in dists if dist in (1, ROW_CHIPS)]
    stages = []
    for dist in starts:
        chain = [(dist, None, dist)]
        while chain[-1][0] * 2 in dists and chain[-1][0] * 2 not in starts:
            chain.append((chain[-1][0] * 2, chain[-1][0], chain[-1][0]))
        stages.append(chain)

    def seq_peer(delta):
        return (lax.rem(seq + (delta + n_seq), n_seq), head)

    def head_peer(delta):
        return (seq, lax.rem(head + delta, n_head))

    loads = [
        pltpu.make_async_copy(k_hbm, k_all.at[0], load_sem.at[0]),
        pltpu.make_async_copy(v_hbm, v_all.at[0], load_sem.at[1]),
        pltpu.make_async_copy(q_hbm, q_all.at[0], load_sem.at[2]),
        pltpu.make_async_copy(w_hbm, w_own, load_sem.at[3]),
        pltpu.make_async_copy(
            g_hbm, g_full.at[:, pl.ds(pl.multiple_of(head * HD, HD), HD)], load_sem.at[4]
        ),
        pltpu.make_async_copy(
            w_hbm.at[:, pl.ds(pl.multiple_of(head * HD, HD), HD)],
            w_col.at[pl.ds(pl.multiple_of(head * HD, HD), HD), :],
            load_sem.at[5],
        ),
    ]
    for load in loads:
        load.start()

    barrier = pltpu.get_barrier_semaphore()
    deltas = sorted({d % n_seq for d in dists} | {(-d) % n_seq for d in dists})
    for delta in deltas:
        pl.semaphore_signal(barrier, inc=1, device_id=seq_peer(delta), device_id_type=MESH)
    for delta in range(1, n_head):
        pl.semaphore_signal(barrier, inc=1, device_id=head_peer(delta), device_id_type=MESH)
    pl.semaphore_wait(barrier, len(deltas) + n_head - 1)

    def seq_copies(number, own, buffer, sign):
        copies = {}
        for chain in stages:
            for dist, source, hop in chain:
                index = number * n_dist + slot_of[dist] - 1
                copies[dist] = pltpu.make_async_remote_copy(
                    src_ref=own if source is None else buffer.at[slot_of[source]],
                    dst_ref=buffer.at[slot_of[dist]],
                    send_sem=seq_send.at[index],
                    recv_sem=seq_recv.at[index],
                    device_id=seq_peer(sign * hop),
                    device_id_type=MESH,
                )
        return copies

    k_copies = seq_copies(0, k_hbm, k_all, 1)
    v_copies = seq_copies(1, v_hbm, v_all, 1)
    q_copies = seq_copies(2, q_hbm, q_all, -1)
    g_copies = seq_copies(3, g_all.at[0], g_all, -1)

    def head_copies(number, source, target):
        return [
            pltpu.make_async_remote_copy(
                src_ref=source(lax.rem(head + delta, n_head)),
                dst_ref=target,
                send_sem=head_send.at[number * (n_head - 1) + delta - 1],
                recv_sem=head_recv.at[number * (n_head - 1) + delta - 1],
                device_id=head_peer(delta),
                device_id_type=MESH,
            )
            for delta in range(1, n_head)
        ]

    my_columns = pl.ds(pl.multiple_of(head * HD, HD), HD)
    out_copies = head_copies(0, lambda peer: g_hbm, g_full.at[:, my_columns])
    w_copies = head_copies(
        1,
        lambda peer: w_hbm.at[:, pl.ds(pl.multiple_of(peer * HD, HD), HD)],
        w_col.at[my_columns, :],
    )
    a_copies = head_copies(2, lambda peer: a_full.at[:, my_columns], a_full.at[:, my_columns])

    def launch(copies):
        for dist in starts:
            copies[dist].start()

    def relay(copies, depth):
        for chain in stages:
            if depth < len(chain):
                copies[chain[depth][0]].wait_recv()
            if depth + 1 < len(chain):
                copies[chain[depth + 1][0]].start()

    most = max(len(chain) for chain in stages)
    launch(k_copies)
    launch(q_copies)
    for copy in out_copies:
        copy.start()
    launch(v_copies)
    for copy in w_copies:
        copy.start()
    for depth in range(most - 1):
        relay(k_copies, depth)
        relay(q_copies, depth)
    for load in loads:
        load.wait()
    for copy in out_copies:
        copy.wait_recv()
    g_own = dot_nt(g_full[...], w_own[...]).astype(jnp.bfloat16)
    for block in range(nb):
        g_all[0, block] = g_own[block * BLOCK : (block + 1) * BLOCK]
    launch(g_copies)
    for depth in range(most - 1):
        relay(v_copies, depth)
        relay(g_copies, depth)
    relay(k_copies, most - 1)
    relay(v_copies, most - 1)

    near = [2**power for power in range(LEVELS) if 2**power < nb]
    far = [(dist, slot_of[dist]) for dist in dists]
    count = 1 + len(near) + len(far)
    width = count * BLOCK
    scaling = HD ** (-0.5)

    def gathered(buffer, block, sign):
        pieces = [buffer[0, block]]
        for stride in near:
            other = block - sign * stride
            pieces.append(buffer[0, other] if 0 <= other < nb else buffer[1, other % nb])
        for _, slot in far:
            pieces.append(buffer[slot, block])
        return jnp.concatenate(pieces, axis=0)

    lanes = lax.broadcasted_iota(jnp.int32, (1, width), 1)
    levels = lanes // BLOCK
    rows = lax.broadcasted_iota(jnp.int32, (BLOCK, width), 0)
    columns = lax.broadcasted_iota(jnp.int32, (BLOCK, width), 1)
    earlier = columns <= rows
    later = (columns >= rows) | (columns >= BLOCK)

    stat_lane = lax.broadcasted_iota(jnp.int32, (BLOCK, HD), 1)
    stats = jnp.zeros((BLOCK, HD), jnp.float32)
    kept = []
    for block in range(nb):
        keys = gathered(k_all, block, 1)
        values = gathered(v_all, block, 1)
        scores = dot_nt(q_all[0, block], keys) * scaling
        flags = jnp.zeros((1, width), jnp.int32)
        for level in range(count - 1):
            flags = jnp.where(levels == level + 1, kb_ref[block : block + 1, level : level + 1], flags)
        allowed = (flags >= 0) & ((columns >= BLOCK) | earlier)
        scores = jnp.where(allowed, scores, -BIG)
        highest = jnp.max(scores, axis=1, keepdims=True)
        powers = jnp.exp(scores - highest)
        total = jnp.sum(powers, axis=1, keepdims=True)
        probs = powers * (1.0 / total)
        log_total = highest + jnp.log(total)
        attn = dot_nn(probs.astype(jnp.bfloat16), values).astype(jnp.bfloat16)
        a_full[block * BLOCK : (block + 1) * BLOCK, my_columns] = attn
        grads = g_all[0, block]
        inner = jnp.sum(grads.astype(jnp.float32) * attn.astype(jnp.float32), axis=1, keepdims=True)
        stats = jnp.where(stat_lane == block, log_total, stats)
        stats = jnp.where(stat_lane == nb + block, inner, stats)
        kept.append((keys, values, probs, inner))
    turned = jnp.concatenate([stats, stats], axis=0).T[0 : 2 * nb]
    stat_mine[0] = turned
    for level in range(count - 1):
        stat_mine[1 + level, 0:nb] = jnp.where(
            kb_ref[:, level : level + 1] >= 0, turned[0:nb], BIG
        )
        stat_mine[1 + level, nb : 2 * nb] = turned[nb : 2 * nb]
    first_far = 1 + len(near)
    stat_copies = []
    for number, (dist, slot) in enumerate(far):
        low = 1 if dist == 1 else first_far + number
        high = first_far + number + 1
        stat_copies.append(
            pltpu.make_async_remote_copy(
                src_ref=stat_mine.at[low:high],
                dst_ref=stat_got.at[low:high],
                send_sem=stat_send.at[number],
                recv_sem=stat_recv.at[number],
                device_id=seq_peer(-dist),
                device_id_type=MESH,
            )
        )
    for copy in reversed(stat_copies):
        copy.start()
    for copy in a_copies:
        copy.start()

    for block in range(nb):
        keys, values, probs, inner = kept[block]
        grad_probs = dot_nt(g_all[0, block], values)
        grad_scores = (probs * (grad_probs - inner) * scaling).astype(jnp.bfloat16)
        dq_ref[block] = dot_nn(grad_scores, keys).astype(jnp.bfloat16)

    relay(q_copies, most - 1)
    relay(g_copies, most - 1)
    for copy in stat_copies:
        copy.wait_recv()

    half = lax.broadcasted_iota(jnp.int32, (1, 2 * BLOCK), 1) < BLOCK
    for block in range(nb):
        sources = [(stat_mine, 0, block)]
        for number, stride in enumerate(near):
            other = block + stride
            inside = other < nb
            sources.append((stat_mine if inside else stat_got, 1 + number, other % nb))
        for number in range(len(far)):
            sources.append((stat_got, first_far + number, block))

        def stat_row(offset):
            pieces = []
            for index in range(0, count, 2):
                ref, level, row = sources[index]
                piece = ref[level, offset + row : offset + row + 1, :]
                if index + 1 < count:
                    ref, level, row = sources[index + 1]
                    piece = jnp.where(half, piece, ref[level, offset + row : offset + row + 1, :])
                else:
                    piece = piece[:, 0:BLOCK]
                pieces.append(piece)
            return jnp.concatenate(pieces, axis=1)

        askers = gathered(q_all, block, -1)
        grads = gathered(g_all, block, -1)
        scores = dot_nt(k_all[0, block], askers) * scaling
        probs = jnp.exp(jnp.where(later, scores - stat_row(0), -BIG))
        dv_ref[block] = dot_nn(probs.astype(jnp.bfloat16), grads).astype(jnp.bfloat16)
        grad_probs = dot_nt(v_all[0, block], grads)
        grad_scores = (probs * (grad_probs - stat_row(nb)) * scaling).astype(jnp.bfloat16)
        dk_ref[block] = dot_nn(grad_scores, askers).astype(jnp.bfloat16)

    for copy in w_copies:
        copy.wait_recv()
    for copy in a_copies:
        copy.wait_recv()
    mixed_ref[...] = dot_nn(a_full[...], w_col[...]).astype(jnp.bfloat16)

    for copies in (k_copies, v_copies, q_copies, g_copies):
        for dist in dists:
            copies[dist].wait_send()
    for copy in out_copies + w_copies + a_copies + stat_copies:
        copy.wait_send()


def per_device(queries, key_rows, value_rows, key_blocks, out_weight, grad_out):
    n_seq, n_head = lax.axis_size("seq"), lax.axis_size("head")
    rows = queries.shape[0]
    width = out_weight.shape[1]
    nb = rows // BLOCK
    dists = [2**power // nb for power in range(LEVELS) if nb <= 2**power < nb * n_seq]
    blocked = (nb, BLOCK, HD)
    slots = (1 + len(dists),) + blocked
    near = [2**power for power in range(LEVELS) if 2**power < nb]
    count = 1 + len(near) + len(dists)
    vmem = pl.BlockSpec(memory_space=pltpu.VMEM)
    hbm = pl.BlockSpec(memory_space=pl.ANY)
    mixed, dq, dk, dv = pl.pallas_call(
        functools.partial(kernel, n_seq, n_head, dists),
        out_shape=[jax.ShapeDtypeStruct((rows, HD), jnp.bfloat16)]
        + [jax.ShapeDtypeStruct(blocked, jnp.bfloat16)] * 3,
        in_specs=[hbm, hbm, hbm, vmem, hbm, hbm],
        out_specs=[vmem] * 4,
        scratch_shapes=[pltpu.VMEM(slots, jnp.bfloat16)] * 4
        + [
            pltpu.VMEM((rows, width), jnp.bfloat16),
            pltpu.VMEM((HD, width), jnp.bfloat16),
            pltpu.VMEM((width, HD), jnp.bfloat16),
            pltpu.VMEM((rows, width), jnp.bfloat16),
            pltpu.VMEM((count, 2 * nb, HD), jnp.float32),
            pltpu.VMEM((count, 2 * nb, HD), jnp.float32),
            pltpu.SemaphoreType.DMA((4 * len(dists),)),
            pltpu.SemaphoreType.DMA((4 * len(dists),)),
            pltpu.SemaphoreType.DMA((3 * (n_head - 1),)),
            pltpu.SemaphoreType.DMA((3 * (n_head - 1),)),
            pltpu.SemaphoreType.DMA((len(dists),)),
            pltpu.SemaphoreType.DMA((len(dists),)),
            pltpu.SemaphoreType.DMA((6,)),
        ],
        compiler_params=pltpu.CompilerParams(collective_id=0, has_side_effects=True),
    )(
        queries.reshape(blocked),
        key_rows.reshape(blocked),
        value_rows.reshape(blocked),
        key_blocks,
        out_weight,
        grad_out,
    )
    flat = (rows, HD)
    return mixed, dq.reshape(flat), dk.reshape(flat), dv.reshape(flat)


def solution(mesh):
    in_specs = (
        P("seq", "head"),
        P("seq", "head"),
        P("seq", "head"),
        P("seq", None),
        P("head", None),
        P("seq", "head"),
    )
    out_specs = (P("seq", "head"), P("seq", "head"), P("seq", "head"), P("seq", "head"))
    return jax.shard_map(
        per_device, mesh=mesh, in_specs=in_specs, out_specs=out_specs, check_vma=False
    )
```

time: 135 us -> 54.5 us (0.40)
  the two profiles are of different devices: /device:TPU:32 before, /device:TPU:1 now
where the time goes in v1:
time: 54.5 us; the launch traced here: 54.2 us
  Pallas kernels  49.7 us (91%)
  local copies, waits for them, and re-layouts  3.86 us (7%)
  between operations  0.65 us (1%)
    pallas_call x1, Pallas kernels, per_device(): pl.pallas_call(functools.partial(kernel, n_seq, n_head, dists), out_shape...  49.7 us
    unnamed x10, local copies, waits for them, and re-layouts  3.86 us

profile of v1, /device:TPU:1, one launch (start us, length us, event | category | flops | bytes accessed | tf_op | source)
XLA Modules:
  0.0 54.2 jit_solution(3589574007202526348)
XLA Ops:
  0.6 49.7 %shard_map.93 = (bf16[256,128]{1,0:T(8,128)(2,1)}, bf16[4,64,128]{2,1,0:T(8,128)(2,1)}, bf16[4,64,128]{2,1,0:T(8,128)(2,1)}, bf16[4,64,128]{2,1,0:T(8,128)(2,1)}) custom-call(bf16[4,64,128]{2,1,0:T(8,128)(2,1)} %bitcast.9, bf16[4,64,128]{2,1,0:T(8,128)(2,1)} %bitcast.10, bf16[4,64,128]{2,1,0:T(8,128)(2,1)} %bitcast.11, s32[4,9]{1,0:T(4,128)} %kb_ref.1, ...), custom_call_target="tpu_custom_call" | custom-call | tf_op jit(solution)/shard_map/pallas_call | solution.py:296
  50.4 0.0 copy-start.2
  50.4 1.5 %copy.14 = bf16[256,128]{1,0:T(8,128)(2,1)} copy(bf16[256,128]{1,0:T(8,128)(2,1)} %get-tuple-element.16) | data formatting | bytes 131072
  51.9 0.0 copy-done.2
  51.9 0.0 copy-start.1
  51.9 0.6 %copy.15 = bf16[256,128]{1,0:T(8,128)(2,1)} copy(bf16[256,128]{1,0:T(8,128)(2,1)S(1)} %bitcast.8) | data formatting | bytes 131072
  52.5 0.2 copy-done.1
  52.7 0.0 copy-start
  52.7 0.6 %copy.16 = bf16[256,128]{1,0:T(8,128)(2,1)} copy(bf16[256,128]{1,0:T(8,128)(2,1)S(1)} %bitcast.7) | data formatting | bytes 131072
  53.4 0.2 copy-done
  53.6 0.6 %copy.17 = bf16[256,128]{1,0:T(8,128)(2,1)} copy(bf16[256,128]{1,0:T(8,128)(2,1)S(1)} %bitcast.6) | data formatting | bytes 131072
Async XLA Ops:
  50.4 1.5 %copy-start.2 = (bf16[4,64,128]{2,1,0:T(8,128)(2,1)S(1)}, bf16[4,64,128]{2,1,0:T(8,128)(2,1)}, u32[]{:S(2)}) copy-start(bf16[4,64,128]{2,1,0:T(8,128)(2,1)} %get-tuple-element.9) | copy-start | bytes 196612
  51.9 0.9 %copy-start.1 = (bf16[4,64,128]{2,1,0:T(8,128)(2,1)S(1)}, bf16[4,64,128]{2,1,0:T(8,128)(2,1)}, u32[]{:S(2)}) copy-start(bf16[4,64,128]{2,1,0:T(8,128)(2,1)} %get-tuple-element.10) | copy-start | bytes 196612
  52.7 0.9 %copy-start = (bf16[4,64,128]{2,1,0:T(8,128)(2,1)S(1)}, bf16[4,64,128]{2,1,0:T(8,128)(2,1)}, u32[]{:S(2)}) copy-start(bf16[4,64,128]{2,1,0:T(8,128)(2,1)} %get-tuple-element.11) | copy-start | bytes 196612

commit v2 on v1

v2 whole, which is shorter than its diff:
```python
import functools

import jax
import jax.numpy as jnp
from jax import lax
from jax.experimental import pallas as pl
from jax.experimental.pallas import tpu as pltpu
from jax.sharding import PartitionSpec as P

HD = 128
BLOCK = 64
LEVELS = 9
ROW = 8
MESH = pl.DeviceIdType.MESH
BIG = 1e30


def dot_nt(a, b):
    return lax.dot_general(a, b, (((1,), (1,)), ((), ())), preferred_element_type=jnp.float32)


def dot_nn(a, b):
    return lax.dot_general(a, b, (((1,), (0,)), ((), ())), preferred_element_type=jnp.float32)


class SeqCopies:
    def __init__(self, number, dists, buffer, sign, seq, head, n_seq, send, recv):
        self.buffer, self.sign, self.dists = buffer, sign, dists
        row, col = seq // ROW, lax.rem(seq, ROW)
        self.along = col if sign > 0 else ROW - 1 - col
        self.slot = {dist: 1 + place for place, dist in enumerate(dists)}
        self.extra = 1 + len(dists)
        neighbour = row * ROW + lax.rem(col + (sign + ROW), ROW)
        is_last = self.along // (ROW - 1)
        jump = lambda hop: lax.rem(seq + (sign * hop + n_seq), n_seq)
        base = number * (len(dists) + 1)

        def copy(source, target, place, device):
            return pltpu.make_async_remote_copy(
                src_ref=buffer.at[source],
                dst_ref=buffer.at[target],
                send_sem=send.at[base + place],
                recv_sem=recv.at[base + place],
                device_id=(device, head),
                device_id_type=MESH,
            )

        self.copies = {}
        for place, dist in enumerate(dists):
            slot = self.slot[dist]
            if dist == 1:
                source, device = is_last * self.slot[ROW], neighbour
            elif dist == 2 and dist < ROW:
                one = self.slot[1]
                source, device = one + is_last * (self.extra - one), neighbour
            elif dist == ROW:
                source, device = 0, jump(ROW)
            elif dist == 2 * ROW:
                source, device = self.slot[ROW], jump(ROW)
            else:
                source, device = self.slot[dist // 2], jump(dist // 2)
            self.copies[dist] = copy(source, slot, place, device)
        self.side = copy(self.slot[ROW], self.extra, len(dists), neighbour)

    def start(self):
        self.copies[ROW].start()

        @pl.when(self.along != ROW - 1)
        def _():
            self.copies[1].start()

    def got_row(self):
        self.copies[ROW].wait_recv()
        if 2 * ROW in self.copies:
            self.copies[2 * ROW].start()

        @pl.when(self.along == ROW - 1)
        def _():
            self.copies[1].start()

        @pl.when(self.along == ROW - 2)
        def _():
            self.side.start()

    def got_one(self):
        self.copies[1].wait_recv()

        @pl.when(self.along != ROW - 1)
        def _():
            self.copies[2].start()

        @pl.when(self.along == ROW - 1)
        def _():
            self.side.wait_recv()
            self.copies[2].start()

    def got(self, dist):
        if dist in self.copies:
            self.copies[dist].wait_recv()

    def send(self, dist):
        if dist in self.copies:
            self.copies[dist].start()

    def finish(self):
        for dist in self.dists:
            self.copies[dist].wait_send()

        @pl.when(self.along == ROW - 2)
        def _():
            self.side.wait_send()


class HeadGather:
    def __init__(self, number, own, buffer, seq, head, n_head, send, recv):
        core = lax.rem(head, 2)
        partner = head + 1 - 2 * core
        toward = 2 - 4 * core
        wrap = lambda value: lax.rem(value + 2 * n_head, n_head)

        def columns(who):
            return buffer.at[:, pl.ds(pl.multiple_of(who * HD, HD), HD)]

        def copy(place, who, device, source=None):
            return pltpu.make_async_remote_copy(
                src_ref=columns(who) if source is None else source,
                dst_ref=columns(who),
                send_sem=send.at[7 * number + place],
                recv_sem=recv.at[7 * number + place],
                device_id=(seq, device),
                device_id_type=MESH,
            )

        self.first = [copy(0, head, partner, own)]
        self.relays, self.passes, self.last = [], [], []
        if n_head == 8:
            self.first.append(copy(1, head, wrap(head + toward), own))
            self.first.append(copy(2, head, wrap(head - toward), own))
            self.relays.append(copy(3, wrap(head - toward), wrap(head + toward)))
            self.passes.append(copy(4, wrap(head - toward), partner))
            self.passes.append(copy(5, wrap(head + toward), partner))
            self.last.append(copy(6, wrap(head + 4), partner))

    def start(self):
        for copy in reversed(self.first):
            copy.start()

    def middle(self):
        if self.relays:
            self.first[1].wait_recv()
            self.relays[0].start()
            self.passes[0].start()
            self.first[2].wait_recv()
            self.passes[1].start()

    def late(self):
        if self.relays:
            self.relays[0].wait_recv()
            self.last[0].start()

    def end(self):
        for copy in self.first[:1] + self.passes + self.last:
            copy.wait_recv()

    def finish(self):
        for copy in self.first + self.relays + self.passes + self.last:
            copy.wait_send()


def kernel(
    n_seq, n_head, dists,
    q_hbm, k_hbm, v_hbm, kb_hbm, w_hbm, g_hbm,
    mixed_ref, dq_ref, dk_ref, dv_ref,
    k_all, v_all, q_all, g_all, g_full, w_own, w_col, a_full, stat_mine, stat_got, kb_ref,
    seq_send, seq_recv, head_send, head_recv, w_send, w_recv, stat_send, stat_recv, load_sem,
):
    seq = lax.axis_index("seq")
    head = lax.axis_index("head")
    nb = q_hbm.shape[0]
    my_columns = pl.ds(pl.multiple_of(head * HD, HD), HD)

    load_pairs = [
        (k_hbm, k_all.at[0]),
        (q_hbm, q_all.at[0]),
        (v_hbm, v_all.at[0]),
        (kb_hbm, kb_ref),
        (w_hbm, w_own),
        (g_hbm, g_full.at[:, my_columns]),
        (w_hbm.at[:, my_columns], w_col.at[my_columns, :]),
    ]
    loads = [
        pltpu.make_async_copy(source, target, load_sem.at[place])
        for place, (source, target) in enumerate(load_pairs)
    ]
    for load in loads:
        load.start()

    row, col = seq // ROW, lax.rem(seq, ROW)
    core = lax.rem(head, 2)
    near_seq = [
        row * ROW + lax.rem(col + 1, ROW),
        row * ROW + lax.rem(col + (ROW - 1), ROW),
    ]
    rows_apart = {ROW % n_seq, -ROW % n_seq}
    near_seq += [lax.rem(seq + apart, n_seq) for apart in sorted(rows_apart)]
    near_head = [head + 1 - 2 * core]
    if n_head == 8:
        near_head += [lax.rem(head + 2, n_head), lax.rem(head + (n_head - 2), n_head)]
    barrier = pltpu.get_barrier_semaphore()
    for peer in near_seq:
        pl.semaphore_signal(barrier, inc=1, device_id=(peer, head), device_id_type=MESH)
    for peer in near_head:
        pl.semaphore_signal(barrier, inc=1, device_id=(seq, peer), device_id_type=MESH)
    pl.semaphore_wait(barrier, len(near_seq) + len(near_head))

    where = (seq, head, n_seq, seq_send, seq_recv)
    keys_in = SeqCopies(0, dists, k_all, 1, *where)
    values_in = SeqCopies(1, dists, v_all, 1, *where)
    askers_in = SeqCopies(2, dists, q_all, -1, *where)
    grads_in = SeqCopies(3, dists, g_all, -1, *where)
    out_gather = HeadGather(0, g_hbm, g_full, seq, head, n_head, head_send, head_recv)
    attn_gather = HeadGather(
        1, a_full.at[:, my_columns], a_full, seq, head, n_head, head_send, head_recv
    )
    w_copies = []
    for delta in range(1, n_head):
        peer = lax.rem(head + delta, n_head)
        w_copies.append(
            pltpu.make_async_remote_copy(
                src_ref=w_hbm.at[:, pl.ds(pl.multiple_of(peer * HD, HD), HD)],
                dst_ref=w_col.at[my_columns, :],
                send_sem=w_send.at[delta - 1],
                recv_sem=w_recv.at[delta - 1],
                device_id=(seq, peer),
                device_id_type=MESH,
            )
        )

    out_gather.start()
    loads[0].wait()
    keys_in.start()
    loads[1].wait()
    askers_in.start()
    loads[2].wait()
    values_in.start()

    keys_in.got_row()
    askers_in.got_row()
    out_gather.middle()
    keys_in.got_one()
    askers_in.got_one()
    values_in.got_row()
    values_in.got_one()
    out_gather.late()
    for load in loads[3:]:
        load.wait()
    out_gather.end()
    for copy in w_copies:
        copy.start()
    g_own = dot_nt(g_full[...], w_own[...]).astype(jnp.bfloat16)
    for block in range(nb):
        g_all[0, block] = g_own[block * BLOCK : (block + 1) * BLOCK]
    grads_in.start()
    for dist in (2, 2 * ROW):
        keys_in.got(dist)
        askers_in.got(dist)
    for dist in (2, 2 * ROW):
        if dist * 2 != ROW:
            keys_in.send(dist * 2)
            askers_in.send(dist * 2)
    for dist in (2, 2 * ROW):
        values_in.got(dist)
        if dist * 2 != ROW:
            values_in.send(dist * 2)
    grads_in.got_row()
    grads_in.got_one()
    for dist in (4, 4 * ROW):
        if dist != ROW:
            keys_in.got(dist)

    near = [2**power for power in range(LEVELS) if 2**power < nb]
    far = [(dist, 1 + place) for place, dist in enumerate(dists)]
    count = 1 + len(near) + len(far)
    width = count * BLOCK
    scaling = HD ** (-0.5)

    def gathered(buffer, block, sign):
        pieces = [buffer[0, block]]
        for stride in near:
            other = block - sign * stride
            pieces.append(buffer[0, other] if 0 <= other < nb else buffer[1, other % nb])
        for _, slot in far:
            pieces.append(buffer[slot, block])
        return jnp.concatenate(pieces, axis=0)

    lanes = lax.broadcasted_iota(jnp.int32, (1, width), 1)
    levels = lanes // BLOCK
    rows = lax.broadcasted_iota(jnp.int32, (BLOCK, width), 0)
    columns = lax.broadcasted_iota(jnp.int32, (BLOCK, width), 1)
    earlier = columns <= rows
    later = (columns >= rows) | (columns >= BLOCK)

    kept = []
    for block in range(nb):
        scores = dot_nt(q_all[0, block], gathered(k_all, block, 1)) * scaling
        flags = jnp.zeros((1, width), jnp.int32)
        for level in range(count - 1):
            flags = jnp.where(levels == level + 1, kb_ref[block : block + 1, level : level + 1], flags)
        allowed = (flags >= 0) & ((columns >= BLOCK) | earlier)
        scores = jnp.where(allowed, scores, -BIG)
        highest = jnp.max(scores, axis=1, keepdims=True)
        powers = jnp.exp(scores - highest)
        total = jnp.sum(powers, axis=1, keepdims=True)
        probs = powers * (1.0 / total)
        log_total = highest + jnp.log(total)
        kept.append((probs, log_total))

    for dist in (2, 2 * ROW):
        grads_in.got(dist)
        if dist * 2 != ROW:
            grads_in.send(dist * 2)
    for dist in (4, 4 * ROW):
        if dist != ROW:
            values_in.got(dist)

    stat_lane = lax.broadcasted_iota(jnp.int32, (BLOCK, HD), 1)
    stats = jnp.zeros((BLOCK, HD), jnp.float32)
    inners = []
    for block in range(nb):
        probs, log_total = kept[block]
        attn = dot_nn(probs.astype(jnp.bfloat16), gathered(v_all, block, 1)).astype(jnp.bfloat16)
        a_full[block * BLOCK : (block + 1) * BLOCK, my_columns] = attn
        grads = g_all[0, block]
        inner = jnp.sum(grads.astype(jnp.float32) * attn.astype(jnp.float32), axis=1, keepdims=True)
        stats = jnp.where(stat_lane == block, log_total, stats)
        stats = jnp.where(stat_lane == nb + block, inner, stats)
        inners.append(inner)
    turned = jnp.concatenate([stats, stats], axis=0).T[0 : 2 * nb]
    stat_mine[0] = turned
    for level in range(count - 1):
        stat_mine[1 + level, 0:nb] = jnp.where(
            kb_ref[:, level : level + 1] >= 0, turned[0:nb], BIG
        )
        stat_mine[1 + level, nb : 2 * nb] = turned[nb : 2 * nb]
    first_far = 1 + len(near)
    stat_copies = []
    for number, (dist, slot) in enumerate(far):
        low = 1 if dist == 1 else first_far + number
        high = first_far + number + 1
        stat_copies.append(
            pltpu.make_async_remote_copy(
                src_ref=stat_mine.at[low:high],
                dst_ref=stat_got.at[low:high],
                send_sem=stat_send.at[number],
                recv_sem=stat_recv.at[number],
                device_id=(lax.rem(seq + (n_seq - dist), n_seq), head),
                device_id_type=MESH,
            )
        )
    for copy in reversed(stat_copies):
        copy.start()
    attn_gather.start()

    for block in range(nb):
        probs, _ = kept[block]
        grad_probs = dot_nt(g_all[0, block], gathered(v_all, block, 1))
        grad_scores = (probs * (grad_probs - inners[block]) * scaling).astype(jnp.bfloat16)
        dq_ref[block] = dot_nn(grad_scores, gathered(k_all, block, 1)).astype(jnp.bfloat16)
        if block == nb // 2:
            attn_gather.middle()

    for dist in (4, 4 * ROW):
        if dist != ROW:
            askers_in.got(dist)
            grads_in.got(dist)
    attn_gather.late()
    for copy in stat_copies:
        copy.wait_recv()

    half = lax.broadcasted_iota(jnp.int32, (1, 2 * BLOCK), 1) < BLOCK
    for block in range(nb):
        sources = [(stat_mine, 0, block)]
        for number, stride in enumerate(near):
            other = block + stride
            inside = other < nb
            sources.append((stat_mine if inside else stat_got, 1 + number, other % nb))
        for number in range(len(far)):
            sources.append((stat_got, first_far + number, block))

        def stat_row(offset):
            pieces = []
            for index in range(0, count, 2):
                ref, level, line = sources[index]
                piece = ref[level, offset + line : offset + line + 1, :]
                if index + 1 < count:
                    ref, level, line = sources[index + 1]
                    piece = jnp.where(half, piece, ref[level, offset + line : offset + line + 1, :])
                else:
                    piece = piece[:, 0:BLOCK]
                pieces.append(piece)
            return jnp.concatenate(pieces, axis=1)

        askers = gathered(q_all, block, -1)
        grads = gathered(g_all, block, -1)
        scores = dot_nt(k_all[0, block], askers) * scaling
        probs = jnp.exp(jnp.where(later, scores - stat_row(0), -BIG))
        dv_ref[block] = dot_nn(probs.astype(jnp.bfloat16), grads).astype(jnp.bfloat16)
        grad_probs = dot_nt(v_all[0, block], grads)
        grad_scores = (probs * (grad_probs - stat_row(nb)) * scaling).astype(jnp.bfloat16)
        dk_ref[block] = dot_nn(grad_scores, askers).astype(jnp.bfloat16)

    for copy in w_copies:
        copy.wait_recv()
    attn_gather.end()
    mixed_ref[...] = dot_nn(a_full[...], w_col[...]).astype(jnp.bfloat16)

    for part in (keys_in, values_in, askers_in, grads_in, out_gather, attn_gather):
        part.finish()
    for copy in w_copies + stat_copies:
        copy.wait_send()


def put_out(*refs):
    count = len(refs) // 2
    for source, target in zip(refs[:count], refs[count:]):
        target[...] = source[...]


def per_device(queries, key_rows, value_rows, key_blocks, out_weight, grad_out):
    n_seq, n_head = lax.axis_size("seq"), lax.axis_size("head")
    rows = queries.shape[0]
    width = out_weight.shape[1]
    nb = rows // BLOCK
    dists = [2**power // nb for power in range(LEVELS) if nb <= 2**power < nb * n_seq]
    blocked = (nb, BLOCK, HD)
    slots = (2 + len(dists),) + blocked
    near = [2**power for power in range(LEVELS) if 2**power < nb]
    count = 1 + len(near) + len(dists)
    vmem = pl.BlockSpec(memory_space=pltpu.VMEM)
    hbm = pl.BlockSpec(memory_space=pltpu.HBM)
    seq_sems = pltpu.SemaphoreType.DMA((4 * (len(dists) + 1),))
    results = pl.pallas_call(
        functools.partial(kernel, n_seq, n_head, dists),
        out_shape=[jax.ShapeDtypeStruct((rows, HD), jnp.bfloat16)]
        + [jax.ShapeDtypeStruct(blocked, jnp.bfloat16)] * 3,
        in_specs=[hbm] * 6,
        out_specs=[vmem] * 4,
        scratch_shapes=[pltpu.VMEM(slots, jnp.bfloat16)] * 4
        + [
            pltpu.VMEM((rows, width), jnp.bfloat16),
            pltpu.VMEM((HD, width), jnp.bfloat16),
            pltpu.VMEM((width, HD), jnp.bfloat16),
            pltpu.VMEM((rows, width), jnp.bfloat16),
            pltpu.VMEM((count, 2 * nb, HD), jnp.float32),
            pltpu.VMEM((count, 2 * nb, HD), jnp.float32),
            pltpu.VMEM(key_blocks.shape, jnp.int32),
            seq_sems,
            seq_sems,
            pltpu.SemaphoreType.DMA((14,)),
            pltpu.SemaphoreType.DMA((14,)),
            pltpu.SemaphoreType.DMA((n_head - 1,)),
            pltpu.SemaphoreType.DMA((n_head - 1,)),
            pltpu.SemaphoreType.DMA((len(dists),)),
            pltpu.SemaphoreType.DMA((len(dists),)),
            pltpu.SemaphoreType.DMA((7,)),
        ],
        compiler_params=pltpu.CompilerParams(
            collective_id=0, has_side_effects=True, vmem_limit_bytes=20 * 2**20
        ),
        name="attention",
    )(
        *[
            pltpu.with_memory_space_constraint(array, pltpu.HBM)
            for array in (
                queries.reshape(blocked),
                key_rows.reshape(blocked),
                value_rows.reshape(blocked),
                key_blocks,
                out_weight,
                grad_out,
            )
        ]
    )
    results = pl.pallas_call(
        put_out,
        out_shape=[jax.ShapeDtypeStruct(result.shape, result.dtype) for result in results],
        in_specs=[vmem] * 4,
        out_specs=[vmem] * 4,
        compiler_params=pltpu.CompilerParams(vmem_limit_bytes=8 * 2**20),
        name="put_out",
    )(*results)
    return tuple(result.reshape(rows, HD) for result in results)


def solution(mesh):
    in_specs = (
        P("seq", "head"),
        P("seq", "head"),
        P("seq", "head"),
        P("seq", None),
        P("head", None),
        P("seq", "head"),
    )
    out_specs = (P("seq", "head"), P("seq", "head"), P("seq", "head"), P("seq", "head"))
    return jax.shard_map(
        per_device, mesh=mesh, in_specs=in_specs, out_specs=out_specs, check_vma=False
    )
```

time: 54.5 us -> 48.6 us (0.89)
  the two profiles are of different devices: /device:TPU:1 before, /device:TPU:16 now
where the time goes in v2:
time: 48.6 us; the launch traced here: 48.4 us
  Pallas kernels  47.8 us (98%)
  between operations  0.64 us (1%)
    pallas_call x1, Pallas kernels, per_device(): pl.pallas_call(functools.partial(kernel, n_seq, n_head, dists), out_shape...  47.1 us

profile of v2, /device:TPU:16, one launch (start us, length us, event | category | flops | bytes accessed | tf_op | source)
XLA Modules:
  0.0 48.4 jit_solution(16693863290147467230)
XLA Ops:
  0.6 47.1 %attention.1 = (bf16[256,128]{1,0:T(8,128)(2,1)S(1)}, bf16[4,64,128]{2,1,0:T(8,128)(2,1)S(1)}, bf16[4,64,128]{2,1,0:T(8,128)(2,1)S(1)}, bf16[4,64,128]{2,1,0:T(8,128)(2,1)S(1)}) custom-call(bf16[4,64,128]{2,1,0:T(8,128)(2,1)} %bitcast.6, bf16[4,64,128]{2,1,0:T(8,128)(2,1)} %bitcast.7, bf16[4,64,128]{2,1,0:T(8,128)(2,1)} %bitcast.8, s32[4,9]{1,0:T(4,128)} %kb_hbm.1, ...), custom_call_target="tpu_custom_call" | custom-call | tf_op jit(solution)/shard_map/attention/pallas_call | solution.py:442
  47.7 0.7 %put_out.1 = (bf16[256,128]{1,0:T(8,128)(2,1)}, bf16[4,64,128]{2,1,0:T(8,128)(2,1)}, bf16[4,64,128]{2,1,0:T(8,128)(2,1)}, bf16[4,64,128]{2,1,0:T(8,128)(2,1)}) custom-call(bf16[256,128]{1,0:T(8,128)(2,1)S(1)} %get-tuple-element.12.refs_0_, bf16[4,64,128]{2,1,0:T(8,128)(2,1)S(1)} %get-tuple-element.13.refs_1_, ...), custom_call_target="tpu_custom_call" | custom-call | tf_op jit(solution)/shard_map/put_out/pallas_call | solution.py:484

commit v3 on v2

--- a/solution.py
+++ b/solution.py
@@ -25,13 +25,14 @@
 
 class SeqCopies:
     def __init__(self, number, dists, buffer, sign, seq, head, n_seq, send, recv):
-        self.buffer, self.sign, self.dists = buffer, sign, dists
-        row, col = seq // ROW, lax.rem(seq, ROW)
-        self.along = col if sign > 0 else ROW - 1 - col
+        self.dists, self.ahead = dists, sign > 0
+        row, self.col = seq // ROW, lax.rem(seq, ROW)
+        along = self.col if sign > 0 else ROW - 1 - self.col
+        self.side_col = ROW - 2 if sign > 0 else 1
         self.slot = {dist: 1 + place for place, dist in enumerate(dists)}
         self.extra = 1 + len(dists)
-        neighbour = row * ROW + lax.rem(col + (sign + ROW), ROW)
-        is_last = self.along // (ROW - 1)
+        neighbour = row * ROW + lax.rem(self.col + (sign + ROW), ROW)
+        is_last = along // (ROW - 1)
         jump = lambda hop: lax.rem(seq + (sign * hop + n_seq), n_seq)
         base = number * (len(dists) + 1)
 
@@ -62,51 +63,38 @@
             self.copies[dist] = copy(source, slot, place, device)
         self.side = copy(self.slot[ROW], self.extra, len(dists), neighbour)
 
+    def when(self, low, high, *steps):
+        @pl.when((self.col >= low) & (self.col <= high))
+        def _():
+            self.do(*steps)
+
+    def do(self, *steps):
+        for step, dist in steps:
+            if dist in self.copies or dist == 0:
+                copy = self.copies[dist] if dist else self.side
+                copy.wait_recv() if step == "w" else copy.start()
+
     def start(self):
-        self.copies[ROW].start()
-
-        @pl.when(self.along != ROW - 1)
-        def _():
-            self.copies[1].start()
+        self.do(("s", ROW))
+        if self.ahead:
+            self.when(0, ROW - 2, ("s", 1))
+        else:
+            self.when(1, ROW - 1, ("s", 1))
 
     def got_row(self):
-        self.copies[ROW].wait_recv()
-        if 2 * ROW in self.copies:
-            self.copies[2 * ROW].start()
-
-        @pl.when(self.along == ROW - 1)
-        def _():
-            self.copies[1].start()
-
-        @pl.when(self.along == ROW - 2)
-        def _():
-            self.side.start()
-
-    def got_one(self):
-        self.copies[1].wait_recv()
-
-        @pl.when(self.along != ROW - 1)
-        def _():
-            self.copies[2].start()
-
-        @pl.when(self.along == ROW - 1)
-        def _():
-            self.side.wait_recv()
-            self.copies[2].start()
-
-    def got(self, dist):
-        if dist in self.copies:
-            self.copies[dist].wait_recv()
-
-    def send(self, dist):
-        if dist in self.copies:
-            self.copies[dist].start()
+        self.do(("w", ROW), ("s", 2 * ROW))
+        self.when(self.side_col, self.side_col, ("s", 0))
+        if self.ahead:
+            self.when(ROW - 1, ROW - 1, ("s", 1))
+
+    def got_far(self):
+        self.do(("w", 2 * ROW), ("s", 4 * ROW))
 
     def finish(self):
         for dist in self.dists:
             self.copies[dist].wait_send()
 
-        @pl.when(self.along == ROW - 2)
+        @pl.when(self.col == self.side_col)
         def _():
             self.side.wait_send()
 
@@ -172,7 +160,7 @@
     q_hbm, k_hbm, v_hbm, kb_hbm, w_hbm, g_hbm,
     mixed_ref, dq_ref, dk_ref, dv_ref,
     k_all, v_all, q_all, g_all, g_full, w_own, w_col, a_full, stat_mine, stat_got, kb_ref,
-    seq_send, seq_recv, head_send, head_recv, w_send, w_recv, stat_send, stat_recv, load_sem,
+    seq_send, seq_recv, head_send, head_recv, w_send, w_recv, stat_send, stat_recv, load_sem, wrap_sem,
 ):
     seq = lax.axis_index("seq")
     head = lax.axis_index("head")
@@ -197,21 +185,50 @@
 
     row, col = seq // ROW, lax.rem(seq, ROW)
     core = lax.rem(head, 2)
-    near_seq = [
-        row * ROW + lax.rem(col + 1, ROW),
-        row * ROW + lax.rem(col + (ROW - 1), ROW),
-    ]
-    rows_apart = {ROW % n_seq, -ROW % n_seq}
-    near_seq += [lax.rem(seq + apart, n_seq) for apart in sorted(rows_apart)]
+    last = ROW - 1
+    in_row = [dist for dist in dists if dist < ROW]
+    four = 4 in in_row
+    barrier = pltpu.get_barrier_semaphore()
+
+    def greet(peer_seq, peer_head, semaphore=barrier):
+        pl.semaphore_signal(
+            semaphore, inc=1, device_id=(peer_seq, peer_head), device_id_type=MESH
+        )
+
+    @pl.when(col < last)
+    def _():
+        greet(seq + 1, head)
+
+    @pl.when(col > 0)
+    def _():
+        greet(seq - 1, head)
+
+    @pl.when(col == 0)
+    def _():
+        greet(seq + last, head)
+
+    if four:
+
+        @pl.when(col < 2)
+        def _():
+            greet(lax.rem(seq + (n_seq - 2), n_seq), head)
+
+    rows_apart = sorted({ROW % n_seq, -ROW % n_seq})
     near_head = [head + 1 - 2 * core]
     if n_head == 8:
         near_head += [lax.rem(head + 2, n_head), lax.rem(head + (n_head - 2), n_head)]
-    barrier = pltpu.get_barrier_semaphore()
-    for peer in near_seq:
-        pl.semaphore_signal(barrier, inc=1, device_id=(peer, head), device_id_type=MESH)
+    for apart in rows_apart:
+        greet(lax.rem(seq + apart, n_seq), head)
     for peer in near_head:
-        pl.semaphore_signal(barrier, inc=1, device_id=(seq, peer), device_id_type=MESH)
-    pl.semaphore_wait(barrier, len(near_seq) + len(near_head))
+        greet(seq, peer)
+    expected = len(rows_apart) + len(near_head) + 2 - (last - col) // last
+    if four:
+        expected = expected + col // (last - 1)
+    pl.semaphore_wait(barrier, expected)
+
+    @pl.when(col == last)
+    def _():
+        greet(seq - last, head, wrap_sem)
 
     where = (seq, head, n_seq, seq_send, seq_recv)
     keys_in = SeqCopies(0, dists, k_all, 1, *where)
@@ -247,10 +264,13 @@
     keys_in.got_row()
     askers_in.got_row()
     out_gather.middle()
-    keys_in.got_one()
-    askers_in.got_one()
+    keys_in.when(1, last - 1, ("w", 1), ("s", 2))
+    keys_in.when(last, last, ("w", 1), ("w", 0), ("s", 2))
+    askers_in.when(0, 0, ("w", 1))
+    askers_in.when(1, last - 1, ("w", 1), ("s", 2))
     values_in.got_row()
-    values_in.got_one()
+    values_in.when(1, last - 1, ("w", 1), ("s", 2))
+    values_in.when(last, last, ("w", 1), ("w", 0), ("s", 2))
     out_gather.late()
     for load in loads[3:]:
         load.wait()
@@ -261,22 +281,41 @@
     for block in range(nb):
         g_all[0, block] = g_own[block * BLOCK : (block + 1) * BLOCK]
     grads_in.start()
-    for dist in (2, 2 * ROW):
-        keys_in.got(dist)
-        askers_in.got(dist)
-    for dist in (2, 2 * ROW):
-        if dist * 2 != ROW:
-            keys_in.send(dist * 2)
-            askers_in.send(dist * 2)
-    for dist in (2, 2 * ROW):
-        values_in.got(dist)
-        if dist * 2 != ROW:
-            values_in.send(dist * 2)
+    two, then = ("w", 2), [("s", 4)] if four else []
+    keys_in.do(("w", 2 * ROW))
+    askers_in.do(("w", 2 * ROW))
+    keys_in.do(("s", 4 * ROW))
+    askers_in.do(("s", 4 * ROW))
+    keys_in.when(2, last, two)
+    askers_in.when(0, last - 2, two)
+    keys_in.when(2, last, *then)
+    askers_in.when(2, last - 2, *then)
+    values_in.got_far()
+    values_in.when(2, last, two, *then)
     grads_in.got_row()
-    grads_in.got_one()
-    for dist in (4, 4 * ROW):
-        if dist != ROW:
-            keys_in.got(dist)
+    askers_in.when(last, last, ("w", 1), ("s", 2))
+
+    @pl.when(col == 0)
+    def _():
+        pl.semaphore_wait(wrap_sem, 1)
+        askers_in.do(("s", 1), ("w", 0), ("s", 2))
+
+    grads_in.when(0, 0, ("w", 1), ("s", 1), ("w", 0), ("s", 2))
+    grads_in.when(1, last - 1, ("w", 1), ("s", 2))
+    askers_in.when(last - 1, last, two, *then)
+    grads_in.when(last, last, ("w", 1), ("s", 2))
+    grads_in.got_far()
+    grads_in.do(two)
+    grads_in.when(2, last, *then)
+    keys_in.when(0, 0, ("w", 1), ("s", 2))
+    values_in.when(0, 0, ("w", 1), ("s", 2))
+    keys_in.when(0, 1, two, *then)
+    askers_in.when(0, 1, *then)
+    values_in.when(0, 1, two, *then)
+    grads_in.when(0, 1, *then)
+    keys_in.do(("w", 4 * ROW))
+    if four:
+        keys_in.do(("w", 4))
 
     near = [2**power for power in range(LEVELS) if 2**power < nb]
     far = [(dist, 1 + place) for place, dist in enumerate(dists)]
@@ -315,13 +354,9 @@
         log_total = highest + jnp.log(total)
         kept.append((probs, log_total))
 
-    for dist in (2, 2 * ROW):
-        grads_in.got(dist)
-        if dist * 2 != ROW:
-            grads_in.send(dist * 2)
-    for dist in (4, 4 * ROW):
-        if dist != ROW:
-            values_in.got(dist)
+    values_in.do(("w", 4 * ROW))
+    if four:
+        values_in.do(("w", 4))
 
     stat_lane = lax.broadcasted_iota(jnp.int32, (BLOCK, HD), 1)
     stats = jnp.zeros((BLOCK, HD), jnp.float32)
@@ -369,10 +404,10 @@
         if block == nb // 2:
             attn_gather.middle()
 
-    for dist in (4, 4 * ROW):
-        if dist != ROW:
-            askers_in.got(dist)
-            grads_in.got(dist)
+    for tensor in (askers_in, grads_in):
+        tensor.do(("w", 4 * ROW))
+        if four:
+            tensor.do(("w", 4))
     attn_gather.late()
     for copy in stat_copies:
         copy.wait_recv()
@@ -463,6 +498,7 @@
             pltpu.SemaphoreType.DMA((len(dists),)),
             pltpu.SemaphoreType.DMA((len(dists),)),
             pltpu.SemaphoreType.DMA((7,)),
+            pltpu.SemaphoreType.REGULAR,
         ],
         compiler_params=pltpu.CompilerParams(
             collective_id=0, has_side_effects=True, vmem_limit_bytes=20 * 2**20

time: 48.6 us -> 46 us (0.947)
  the two profiles are of different devices: /device:TPU:16 before, /device:TPU:1 now
where the time goes in v3:
time: 46 us; the launch traced here: 45.9 us
  Pallas kernels  45.2 us (98%)
  between operations  0.64 us (1%)
    pallas_call x1, Pallas kernels, per_device(): pl.pallas_call(functools.partial(kernel, n_seq, n_head, dists), out_shape...  44.5 us

profile of v3, /device:TPU:1, one launch (start us, length us, event | category | flops | bytes accessed | tf_op | source)
XLA Modules:
  0.0 45.9 jit_solution(13155622236920082931)
XLA Ops:
  0.6 44.5 %attention.1 = (bf16[256,128]{1,0:T(8,128)(2,1)S(1)}, bf16[4,64,128]{2,1,0:T(8,128)(2,1)S(1)}, bf16[4,64,128]{2,1,0:T(8,128)(2,1)S(1)}, bf16[4,64,128]{2,1,0:T(8,128)(2,1)S(1)}) custom-call(bf16[4,64,128]{2,1,0:T(8,128)(2,1)} %bitcast.6, bf16[4,64,128]{2,1,0:T(8,128)(2,1)} %bitcast.7, bf16[4,64,128]{2,1,0:T(8,128)(2,1)} %bitcast.8, s32[4,9]{1,0:T(4,128)} %kb_hbm.1, ...), custom_call_target="tpu_custom_call" | custom-call | tf_op jit(solution)/shard_map/attention/pallas_call | solution.py:477
  45.2 0.7 %put_out.1 = (bf16[256,128]{1,0:T(8,128)(2,1)}, bf16[4,64,128]{2,1,0:T(8,128)(2,1)}, bf16[4,64,128]{2,1,0:T(8,128)(2,1)}, bf16[4,64,128]{2,1,0:T(8,128)(2,1)}) custom-call(bf16[256,128]{1,0:T(8,128)(2,1)S(1)} %get-tuple-element.12.refs_0_, bf16[4,64,128]{2,1,0:T(8,128)(2,1)S(1)} %get-tuple-element.13.refs_1_, ...), custom_call_target="tpu_custom_call" | custom-call | tf_op jit(solution)/shard_map/put_out/pallas_call | solution.py:520

commit v4 on v3

--- a/solution.py
+++ b/solution.py
@@ -24,17 +24,14 @@
 
 
 class SeqCopies:
-    def __init__(self, number, dists, buffer, sign, seq, head, n_seq, send, recv):
+    def __init__(self, number, dists, buffer, sign, seq, head, n_seq, send, recv, straight=False):
         self.dists, self.ahead = dists, sign > 0
         row, self.col = seq // ROW, lax.rem(seq, ROW)
         along = self.col if sign > 0 else ROW - 1 - self.col
-        self.side_col = ROW - 2 if sign > 0 else 1
         self.slot = {dist: 1 + place for place, dist in enumerate(dists)}
-        self.extra = 1 + len(dists)
-        neighbour = row * ROW + lax.rem(self.col + (sign + ROW), ROW)
-        is_last = along // (ROW - 1)
+        in_row = lambda hop: row * ROW + lax.rem(self.col + (sign * hop + ROW), ROW)
         jump = lambda hop: lax.rem(seq + (sign * hop + n_seq), n_seq)
-        base = number * (len(dists) + 1)
+        base = number * len(dists)
 
         def copy(source, target, place, device):
             return pltpu.make_async_remote_copy(
@@ -49,19 +46,17 @@
         self.copies = {}
         for place, dist in enumerate(dists):
             slot = self.slot[dist]
-            if dist == 1:
-                source, device = is_last * self.slot[ROW], neighbour
-            elif dist == 2 and dist < ROW:
-                one = self.slot[1]
-                source, device = one + is_last * (self.extra - one), neighbour
+            if dist <= 2:
+                source, device = along // (ROW - dist) * self.slot[ROW], in_row(dist)
             elif dist == ROW:
                 source, device = 0, jump(ROW)
+            elif dist == 2 * ROW and straight:
+                source, device = 0, jump(2 * ROW)
             elif dist == 2 * ROW:
                 source, device = self.slot[ROW], jump(ROW)
             else:
                 source, device = self.slot[dist // 2], jump(dist // 2)
             self.copies[dist] = copy(source, slot, place, device)
-        self.side = copy(self.slot[ROW], self.extra, len(dists), neighbour)
 
     def when(self, low, high, *steps):
         @pl.when((self.col >= low) & (self.col <= high))
@@ -70,33 +65,13 @@
 
     def do(self, *steps):
         for step, dist in steps:
-            if dist in self.copies or dist == 0:
-                copy = self.copies[dist] if dist else self.side
+            if dist in self.copies:
+                copy = self.copies[dist]
                 copy.wait_recv() if step == "w" else copy.start()
-
-    def start(self):
-        self.do(("s", ROW))
-        if self.ahead:
-            self.when(0, ROW - 2, ("s", 1))
-        else:
-            self.when(1, ROW - 1, ("s", 1))
-
-    def got_row(self):
-        self.do(("w", ROW), ("s", 2 * ROW))
-        self.when(self.side_col, self.side_col, ("s", 0))
-        if self.ahead:
-            self.when(ROW - 1, ROW - 1, ("s", 1))
-
-    def got_far(self):
-        self.do(("w", 2 * ROW), ("s", 4 * ROW))
 
     def finish(self):
         for dist in self.dists:
             self.copies[dist].wait_send()
-
-        @pl.when(self.col == self.side_col)
-        def _():
-            self.side.wait_send()
 
 
 class HeadGather:
@@ -160,7 +135,7 @@
     q_hbm, k_hbm, v_hbm, kb_hbm, w_hbm, g_hbm,
     mixed_ref, dq_ref, dk_ref, dv_ref,
     k_all, v_all, q_all, g_all, g_full, w_own, w_col, a_full, stat_mine, stat_got, kb_ref,
-    seq_send, seq_recv, head_send, head_recv, w_send, w_recv, stat_send, stat_recv, load_sem, wrap_sem,
+    seq_send, seq_recv, head_send, head_recv, w_send, w_recv, stat_send, stat_recv, load_sem, ready_sems,
 ):
     seq = lax.axis_index("seq")
     head = lax.axis_index("head")
@@ -207,6 +182,14 @@
     def _():
         greet(seq + last, head)
 
+    @pl.when(col < last - 1)
+    def _():
+        greet(seq + 2, head)
+
+    @pl.when(col < 2)
+    def _():
+        greet(seq + (last - 1), head)
+
     if four:
 
         @pl.when(col < 2)
@@ -221,20 +204,28 @@
         greet(lax.rem(seq + apart, n_seq), head)
     for peer in near_head:
         greet(seq, peer)
-    expected = len(rows_apart) + len(near_head) + 2 - (last - col) // last
-    if four:
-        expected = expected + col // (last - 1)
+    expected = len(rows_apart) + len(near_head) + 3
+    expected = expected - (last - col) // last - (last - col) // (last - 1)
+    expected = expected + (2 if four else 1) * (col // (last - 1))
     pl.semaphore_wait(barrier, expected)
 
     @pl.when(col == last)
     def _():
-        greet(seq - last, head, wrap_sem)
+        greet(seq - last, head, ready_sems.at[0])
+
+    @pl.when(col > last - 2)
+    def _():
+        greet(seq - (last - 1), head, ready_sems.at[1])
+
+    @pl.when(col > 1)
+    def _():
+        greet(seq - 2, head, ready_sems.at[2])
 
     where = (seq, head, n_seq, seq_send, seq_recv)
     keys_in = SeqCopies(0, dists, k_all, 1, *where)
     values_in = SeqCopies(1, dists, v_all, 1, *where)
     askers_in = SeqCopies(2, dists, q_all, -1, *where)
-    grads_in = SeqCopies(3, dists, g_all, -1, *where)
+    grads_in = SeqCopies(3, dists, g_all, -1, *where, straight=True)
     out_gather = HeadGather(0, g_hbm, g_full, seq, head, n_head, head_send, head_recv)
     attn_gather = HeadGather(
         1, a_full.at[:, my_columns], a_full, seq, head, n_head, head_send, head_recv
@@ -253,67 +244,78 @@
             )
         )
 
+    then = [("s", 4)] if four else []
+    two = ("w", 2)
     out_gather.start()
     loads[0].wait()
-    keys_in.start()
+    keys_in.do(("s", ROW))
+    keys_in.when(0, last - 1, ("s", 1))
     loads[1].wait()
-    askers_in.start()
+    askers_in.do(("s", ROW))
+    askers_in.when(1, last, ("s", 1))
+    askers_in.when(2, last, ("s", 2))
     loads[2].wait()
-    values_in.start()
-
-    keys_in.got_row()
-    askers_in.got_row()
+    values_in.do(("s", ROW))
+
+    @pl.when(col < last - 1)
+    def _():
+        pl.semaphore_wait(ready_sems.at[2], 1)
+        keys_in.do(("s", 2))
+
+    values_in.when(0, last - 1, ("s", 1))
+    values_in.when(0, last - 2, ("s", 2))
+
+    keys_in.do(("w", ROW), ("s", 2 * ROW))
+    keys_in.when(last, last, ("s", 1))
+    keys_in.when(last - 1, last, ("s", 2))
+    askers_in.do(("w", ROW), ("s", 2 * ROW))
     out_gather.middle()
-    keys_in.when(1, last - 1, ("w", 1), ("s", 2))
-    keys_in.when(last, last, ("w", 1), ("w", 0), ("s", 2))
-    askers_in.when(0, 0, ("w", 1))
-    askers_in.when(1, last - 1, ("w", 1), ("s", 2))
-    values_in.got_row()
-    values_in.when(1, last - 1, ("w", 1), ("s", 2))
-    values_in.when(last, last, ("w", 1), ("w", 0), ("s", 2))
+    values_in.do(("w", ROW), ("s", 2 * ROW))
+    values_in.when(last, last, ("s", 1))
+    values_in.when(last - 1, last, ("s", 2))
+    keys_in.when(2, last, two, *then)
+    askers_in.when(0, last - 2, two)
+    askers_in.when(2, last - 2, *then)
     out_gather.late()
     for load in loads[3:]:
         load.wait()
     out_gather.end()
-    for copy in w_copies:
-        copy.start()
     g_own = dot_nt(g_full[...], w_own[...]).astype(jnp.bfloat16)
     for block in range(nb):
         g_all[0, block] = g_own[block * BLOCK : (block + 1) * BLOCK]
-    grads_in.start()
-    two, then = ("w", 2), [("s", 4)] if four else []
-    keys_in.do(("w", 2 * ROW))
-    askers_in.do(("w", 2 * ROW))
-    keys_in.do(("s", 4 * ROW))
-    askers_in.do(("s", 4 * ROW))
-    keys_in.when(2, last, two)
-    askers_in.when(0, last - 2, two)
-    keys_in.when(2, last, *then)
-    askers_in.when(2, last - 2, *then)
-    values_in.got_far()
+    keys_in.do(("w", 2 * ROW), ("s", 4 * ROW))
+    askers_in.do(("w", 2 * ROW), ("s", 4 * ROW))
+    grads_in.do(("s", ROW))
+    grads_in.when(1, last, ("s", 1))
+    grads_in.when(2, last, ("s", 2))
+    grads_in.do(("s", 2 * ROW))
+    for copy in w_copies:
+        copy.start()
     values_in.when(2, last, two, *then)
-    grads_in.got_row()
-    askers_in.when(last, last, ("w", 1), ("s", 2))
+    values_in.do(("w", 2 * ROW), ("s", 4 * ROW))
 
     @pl.when(col == 0)
     def _():
-        pl.semaphore_wait(wrap_sem, 1)
-        askers_in.do(("s", 1), ("w", 0), ("s", 2))
-
-    grads_in.when(0, 0, ("w", 1), ("s", 1), ("w", 0), ("s", 2))
-    grads_in.when(1, last - 1, ("w", 1), ("s", 2))
+        pl.semaphore_wait(ready_sems.at[0], 1)
+        askers_in.do(("s", 1))
+
+    @pl.when(col < 2)
+    def _():
+        pl.semaphore_wait(ready_sems.at[1], 1)
+        askers_in.do(("s", 2))
+
     askers_in.when(last - 1, last, two, *then)
-    grads_in.when(last, last, ("w", 1), ("s", 2))
-    grads_in.got_far()
+    grads_in.do(("w", ROW))
+    grads_in.when(0, 0, ("s", 1))
+    grads_in.when(0, 1, ("s", 2))
+    grads_in.do(("w", 2 * ROW), ("s", 4 * ROW))
     grads_in.do(two)
     grads_in.when(2, last, *then)
-    keys_in.when(0, 0, ("w", 1), ("s", 2))
-    values_in.when(0, 0, ("w", 1), ("s", 2))
     keys_in.when(0, 1, two, *then)
     askers_in.when(0, 1, *then)
     values_in.when(0, 1, two, *then)
     grads_in.when(0, 1, *then)
-    keys_in.do(("w", 4 * ROW))
+    keys_in.do(("w", 1), ("w", 4 * ROW))
     if four:
         keys_in.do(("w", 4))
 
@@ -354,7 +356,7 @@
         log_total = highest + jnp.log(total)
         kept.append((probs, log_total))
 
-    values_in.do(("w", 4 * ROW))
+    values_in.do(("w", 1), ("w", 4 * ROW))
     if four:
         values_in.do(("w", 4))
 
@@ -405,7 +407,7 @@
             attn_gather.middle()
 
     for tensor in (askers_in, grads_in):
-        tensor.do(("w", 4 * ROW))
+        tensor.do(("w", 1), ("w", 4 * ROW))
         if four:
             tensor.do(("w", 4))
     attn_gather.late()
@@ -468,12 +470,12 @@
     nb = rows // BLOCK
     dists = [2**power // nb for power in range(LEVELS) if nb <= 2**power < nb * n_seq]
     blocked = (nb, BLOCK, HD)
-    slots = (2 + len(dists),) + blocked
+    slots = (1 + len(dists),) + blocked
     near = [2**power for power in range(LEVELS) if 2**power < nb]
     count = 1 + len(near) + len(dists)
     vmem = pl.BlockSpec(memory_space=pltpu.VMEM)
     hbm = pl.BlockSpec(memory_space=pltpu.HBM)
-    seq_sems = pltpu.SemaphoreType.DMA((4 * (len(dists) + 1),))
+    seq_sems = pltpu.SemaphoreType.DMA((4 * len(dists),))
     results = pl.pallas_call(
         functools.partial(kernel, n_seq, n_head, dists),
         out_shape=[jax.ShapeDtypeStruct((rows, HD), jnp.bfloat16)]
@@ -498,7 +500,7 @@
             pltpu.SemaphoreType.DMA((len(dists),)),
             pltpu.SemaphoreType.DMA((len(dists),)),
             pltpu.SemaphoreType.DMA((7,)),
-            pltpu.SemaphoreType.REGULAR,
+            pltpu.SemaphoreType.REGULAR((3,)),
         ],
         compiler_params=pltpu.CompilerParams(
             collective_id=0, has_side_effects=True, vmem_limit_bytes=20 * 2**20

time: 46 us -> 43.6 us (0.948)
  Pallas kernels: 45.2 us -> 42.6 us
    pallas_call x1, Pallas kernels: 44.5 us -> 41.8 us  [per_device(): pl.pallas_call(functools.partial(kernel, n_seq, n_head, dists), out_shape...]
where the time goes in v4:
time: 43.6 us; the launch traced here: 43.2 us
  Pallas kernels  42.6 us (98%)
  between operations  0.64 us (1%)
    pallas_call x1, Pallas kernels, per_device(): pl.pallas_call(functools.partial(kernel, n_seq, n_head, dists), out_shape...  41.8 us

profile of v4, /device:TPU:1, one launch (start us, length us, event | category | flops | bytes accessed | tf_op | source)
XLA Modules:
  0.0 43.2 jit_solution(151602115435163408)
XLA Ops:
  0.6 41.8 %attention.1 = (bf16[256,128]{1,0:T(8,128)(2,1)S(1)}, bf16[4,64,128]{2,1,0:T(8,128)(2,1)S(1)}, bf16[4,64,128]{2,1,0:T(8,128)(2,1)S(1)}, bf16[4,64,128]{2,1,0:T(8,128)(2,1)S(1)}) custom-call(bf16[4,64,128]{2,1,0:T(8,128)(2,1)} %bitcast.6, bf16[4,64,128]{2,1,0:T(8,128)(2,1)} %bitcast.7, bf16[4,64,128]{2,1,0:T(8,128)(2,1)} %bitcast.8, s32[4,9]{1,0:T(4,128)} %kb_hbm.1, ...), custom_call_target="tpu_custom_call" | custom-call | tf_op jit(solution)/shard_map/attention/pallas_call | solution.py:479
  42.5 0.7 %put_out.1 = (bf16[256,128]{1,0:T(8,128)(2,1)}, bf16[4,64,128]{2,1,0:T(8,128)(2,1)}, bf16[4,64,128]{2,1,0:T(8,128)(2,1)}, bf16[4,64,128]{2,1,0:T(8,128)(2,1)}) custom-call(bf16[256,128]{1,0:T(8,128)(2,1)S(1)} %get-tuple-element.12.refs_0_, bf16[4,64,128]{2,1,0:T(8,128)(2,1)S(1)} %get-tuple-element.13.refs_1_, ...), custom_call_target="tpu_custom_call" | custom-call | tf_op jit(solution)/shard_map/put_out/pallas_call | solution.py:522

commit v5 on v4

--- a/solution.py
+++ b/solution.py
@@ -24,10 +24,9 @@
 
 
 class SeqCopies:
-    def __init__(self, number, dists, buffer, sign, seq, head, n_seq, send, recv, straight=False):
+    def __init__(self, number, dists, buffer, sign, seq, head, n_seq, send, recv, own, straight=False):
         self.dists, self.ahead = dists, sign > 0
         row, self.col = seq // ROW, lax.rem(seq, ROW)
-        along = self.col if sign > 0 else ROW - 1 - self.col
         self.slot = {dist: 1 + place for place, dist in enumerate(dists)}
         in_row = lambda hop: row * ROW + lax.rem(self.col + (sign * hop + ROW), ROW)
         jump = lambda hop: lax.rem(seq + (sign * hop + n_seq), n_seq)
@@ -35,7 +34,7 @@
 
         def copy(source, target, place, device):
             return pltpu.make_async_remote_copy(
-                src_ref=buffer.at[source],
+                src_ref=source,
                 dst_ref=buffer.at[target],
                 send_sem=send.at[base + place],
                 recv_sem=recv.at[base + place],
@@ -43,11 +42,11 @@
                 device_id_type=MESH,
             )
 
-        self.copies = {}
+        self.copies, self.firsts = {}, {}
         for place, dist in enumerate(dists):
             slot = self.slot[dist]
             if dist <= 2:
-                source, device = along // (ROW - dist) * self.slot[ROW], in_row(dist)
+                source, device = self.slot[ROW], in_row(dist)
             elif dist == ROW:
                 source, device = 0, jump(ROW)
             elif dist == 2 * ROW and straight:
@@ -56,7 +55,8 @@
                 source, device = self.slot[ROW], jump(ROW)
             else:
                 source, device = self.slot[dist // 2], jump(dist // 2)
-            self.copies[dist] = copy(source, slot, place, device)
+            self.copies[dist] = copy(buffer.at[source], slot, place, device)
+            self.firsts[dist] = copy(own, slot, place, device)
 
     def when(self, low, high, *steps):
         @pl.when((self.col >= low) & (self.col <= high))
@@ -66,7 +66,7 @@
     def do(self, *steps):
         for step, dist in steps:
             if dist in self.copies:
-                copy = self.copies[dist]
+                copy = (self.firsts if step == "o" else self.copies)[dist]
                 copy.wait_recv() if step == "w" else copy.start()
 
     def finish(self):
@@ -99,7 +99,8 @@
         if n_head == 8:
             self.first.append(copy(1, head, wrap(head + toward), own))
             self.first.append(copy(2, head, wrap(head - toward), own))
-            self.relays.append(copy(3, wrap(head - toward), wrap(head + toward)))
+            self.first.append(copy(3, head, wrap(head + 4), own))
+            self.relays.append(self.first[3])
             self.passes.append(copy(4, wrap(head - toward), partner))
             self.passes.append(copy(5, wrap(head + toward), partner))
             self.last.append(copy(6, wrap(head + 4), partner))
@@ -111,7 +112,6 @@
     def middle(self):
         if self.relays:
             self.first[1].wait_recv()
-            self.relays[0].start()
             self.passes[0].start()
             self.first[2].wait_recv()
             self.passes[1].start()
@@ -126,7 +126,7 @@
             copy.wait_recv()
 
     def finish(self):
-        for copy in self.first + self.relays + self.passes + self.last:
+        for copy in self.first + self.passes + self.last:
             copy.wait_send()
 
 
@@ -199,7 +199,7 @@
     rows_apart = sorted({ROW % n_seq, -ROW % n_seq})
     near_head = [head + 1 - 2 * core]
     if n_head == 8:
-        near_head += [lax.rem(head + 2, n_head), lax.rem(head + (n_head - 2), n_head)]
+        near_head += [lax.rem(head + hop, n_head) for hop in (2, 4, 6)]
     for apart in rows_apart:
         greet(lax.rem(seq + apart, n_seq), head)
     for peer in near_head:
@@ -222,10 +222,10 @@
         greet(seq - 2, head, ready_sems.at[2])
 
     where = (seq, head, n_seq, seq_send, seq_recv)
-    keys_in = SeqCopies(0, dists, k_all, 1, *where)
-    values_in = SeqCopies(1, dists, v_all, 1, *where)
-    askers_in = SeqCopies(2, dists, q_all, -1, *where)
-    grads_in = SeqCopies(3, dists, g_all, -1, *where, straight=True)
+    keys_in = SeqCopies(0, dists, k_all, 1, *where, k_hbm)
+    values_in = SeqCopies(1, dists, v_all, 1, *where, v_hbm)
+    askers_in = SeqCopies(2, dists, q_all, -1, *where, q_hbm)
+    grads_in = SeqCopies(3, dists, g_all, -1, *where, g_all.at[0], straight=True)
     out_gather = HeadGather(0, g_hbm, g_full, seq, head, n_head, head_send, head_recv)
     attn_gather = HeadGather(
         1, a_full.at[:, my_columns], a_full, seq, head, n_head, head_send, head_recv
@@ -246,24 +246,21 @@
 
     then = [("s", 4)] if four else []
     two = ("w", 2)
+    keys_in.do(("o", ROW))
+    keys_in.when(0, last - 1, ("o", 1))
+    askers_in.do(("o", ROW))
+    askers_in.when(1, last, ("o", 1))
+    askers_in.when(2, last, ("o", 2))
     out_gather.start()
-    loads[0].wait()
-    keys_in.do(("s", ROW))
-    keys_in.when(0, last - 1, ("s", 1))
-    loads[1].wait()
-    askers_in.do(("s", ROW))
-    askers_in.when(1, last, ("s", 1))
-    askers_in.when(2, last, ("s", 2))
-    loads[2].wait()
-    values_in.do(("s", ROW))
+    values_in.do(("o", ROW))
 
     @pl.when(col < last - 1)
     def _():
         pl.semaphore_wait(ready_sems.at[2], 1)
-        keys_in.do(("s", 2))
-
-    values_in.when(0, last - 1, ("s", 1))
-    values_in.when(0, last - 2, ("s", 2))
+        keys_in.do(("o", 2))
+
+    values_in.when(0, last - 1, ("o", 1))
+    values_in.when(0, last - 2, ("o", 2))
 
     keys_in.do(("w", ROW), ("s", 2 * ROW))
     keys_in.when(last, last, ("s", 1))
@@ -277,7 +274,7 @@
     askers_in.when(0, last - 2, two)
     askers_in.when(2, last - 2, *then)
     out_gather.late()
-    for load in loads[3:]:
+    for load in loads:
         load.wait()
     out_gather.end()
     g_own = dot_nt(g_full[...], w_own[...]).astype(jnp.bfloat16)
@@ -285,10 +282,10 @@
         g_all[0, block] = g_own[block * BLOCK : (block + 1) * BLOCK]
     keys_in.do(("w", 2 * ROW), ("s", 4 * ROW))
     askers_in.do(("w", 2 * ROW), ("s", 4 * ROW))
-    grads_in.do(("s", ROW))
-    grads_in.when(1, last, ("s", 1))
-    grads_in.when(2, last, ("s", 2))
-    grads_in.do(("s", 2 * ROW))
+    grads_in.do(("o", ROW))
+    grads_in.when(1, last, ("o", 1))
+    grads_in.when(2, last, ("o", 2))
+    grads_in.do(("o", 2 * ROW))
     for copy in w_copies:
         copy.start()
     values_in.when(2, last, two, *then)
@@ -308,12 +305,12 @@
     grads_in.do(("w", ROW))
     grads_in.when(0, 0, ("s", 1))
     grads_in.when(0, 1, ("s", 2))
+    keys_in.when(0, 1, two, *then)
+    askers_in.when(0, 1, *then)
+    values_in.when(0, 1, two, *then)
     grads_in.do(("w", 2 * ROW), ("s", 4 * ROW))
     grads_in.do(two)
     grads_in.when(2, last, *then)
-    keys_in.when(0, 1, two, *then)
-    askers_in.when(0, 1, *then)
-    values_in.when(0, 1, two, *then)
     grads_in.when(0, 1, *then)
     keys_in.do(("w", 1), ("w", 4 * ROW))
     if four:
@@ -372,6 +369,7 @@
         stats = jnp.where(stat_lane == block, log_total, stats)
         stats = jnp.where(stat_lane == nb + block, inner, stats)
         inners.append(inner)
+    attn_gather.start()
     turned = jnp.concatenate([stats, stats], axis=0).T[0 : 2 * nb]
     stat_mine[0] = turned
     for level in range(count - 1):
@@ -396,21 +394,30 @@
         )
     for copy in reversed(stat_copies):
         copy.start()
-    attn_gather.start()
 
     for block in range(nb):
         probs, _ = kept[block]
         grad_probs = dot_nt(g_all[0, block], gathered(v_all, block, 1))
         grad_scores = (probs * (grad_probs - inners[block]) * scaling).astype(jnp.bfloat16)
         dq_ref[block] = dot_nn(grad_scores, gathered(k_all, block, 1)).astype(jnp.bfloat16)
-        if block == nb // 2:
-            attn_gather.middle()
-
+
+    attn_gather.middle()
+    attn_gather.late()
     for tensor in (askers_in, grads_in):
         tensor.do(("w", 1), ("w", 4 * ROW))
         if four:
             tensor.do(("w", 4))
-    attn_gather.late()
+    drafts = []
+    for block in range(nb):
+        askers = gathered(q_all, block, -1)
+        grads = gathered(g_all, block, -1)
+        drafts.append(
+            (dot_nt(k_all[0, block], askers) * scaling, dot_nt(v_all[0, block], grads))
+        )
+    for copy in w_copies:
+        copy.wait_recv()
+    attn_gather.end()
+    mixed_ref[...] = dot_nn(a_full[...], w_col[...]).astype(jnp.bfloat16)
     for copy in stat_copies:
         copy.wait_recv()
 
@@ -439,17 +446,11 @@
 
         askers = gathered(q_all, block, -1)
         grads = gathered(g_all, block, -1)
-        scores = dot_nt(k_all[0, block], askers) * scaling
+        scores, grad_probs = drafts[block]
         probs = jnp.exp(jnp.where(later, scores - stat_row(0), -BIG))
         dv_ref[block] = dot_nn(probs.astype(jnp.bfloat16), grads).astype(jnp.bfloat16)
-        grad_probs = dot_nt(v_all[0, block], grads)
         grad_scores = (probs * (grad_probs - stat_row(nb)) * scaling).astype(jnp.bfloat16)
         dk_ref[block] = dot_nn(grad_scores, askers).astype(jnp.bfloat16)
-
-    for copy in w_copies:
-        copy.wait_recv()
-    attn_gather.end()
-    mixed_ref[...] = dot_nn(a_full[...], w_col[...]).astype(jnp.bfloat16)
 
     for part in (keys_in, values_in, askers_in, grads_in, out_gather, attn_gather):
         part.finish()

time: 43.6 us -> 42 us (0.963)
  Pallas kernels: 42.6 us -> 41.2 us
    pallas_call x1, Pallas kernels: 41.8 us -> 40.5 us  [per_device(): pl.pallas_call(functools.partial(kernel, n_seq, n_head, dists), out_shape...]
where the time goes in v5:
time: 42 us; the launch traced here: 41.8 us
  Pallas kernels  41.2 us (98%)
  between operations  0.64 us (2%)
    pallas_call x1, Pallas kernels, per_device(): pl.pallas_call(functools.partial(kernel, n_seq, n_head, dists), out_shape...  40.5 us

profile of v5, /device:TPU:1, one launch (start us, length us, event | category | flops | bytes accessed | tf_op | source)
XLA Modules:
  0.0 41.8 jit_solution(7903218292403867109)
XLA Ops:
  0.6 40.5 %attention.1 = (bf16[256,128]{1,0:T(8,128)(2,1)S(1)}, bf16[4,64,128]{2,1,0:T(8,128)(2,1)S(1)}, bf16[4,64,128]{2,1,0:T(8,128)(2,1)S(1)}, bf16[4,64,128]{2,1,0:T(8,128)(2,1)S(1)}) custom-call(bf16[4,64,128]{2,1,0:T(8,128)(2,1)} %bitcast.6, bf16[4,64,128]{2,1,0:T(8,128)(2,1)} %bitcast.7, bf16[4,64,128]{2,1,0:T(8,128)(2,1)} %bitcast.8, s32[4,9]{1,0:T(4,128)} %kb_hbm.1, ...), custom_call_target="tpu_custom_call" | custom-call | tf_op jit(solution)/shard_map/attention/pallas_call | solution.py:480
  41.1 0.7 %put_out.1 = (bf16[256,128]{1,0:T(8,128)(2,1)}, bf16[4,64,128]{2,1,0:T(8,128)(2,1)}, bf16[4,64,128]{2,1,0:T(8,128)(2,1)}, bf16[4,64,128]{2,1,0:T(8,128)(2,1)}) custom-call(bf16[256,128]{1,0:T(8,128)(2,1)S(1)} %get-tuple-element.12.refs_0_, bf16[4,64,128]{2,1,0:T(8,128)(2,1)S(1)} %get-tuple-element.13.refs_1_, ...), custom_call_target="tpu_custom_call" | custom-call | tf_op jit(solution)/shard_map/put_out/pallas_call | solution.py:523
